TPU v7x, 32 devices: a whole 2x2x4 slice. The times are simulated.
32 devices in a mesh: rep: 2 (over y), ctx: 4 (over z), ch: 2 (over x), sub: 2 (over core).
Axes of the slice: x: 2, y: 2, z: 4, core: 2. Of those that a mesh axis runs over, the one named last changes fastest.
Arguments:
- hyena_query: bfloat16 [3072, 8192], P(('rep', 'ctx'), ('ch', 'sub')), parts along dimension 0, may hold values from -6 to 6
- hyena_key: bfloat16 [3072, 8192], P(('rep', 'ctx'), ('ch', 'sub')), parts along dimension 0, may hold values from -6 to 6
- hyena_value: bfloat16 [3072, 8192], P(('rep', 'ctx'), ('ch', 'sub')), parts along dimension 0, may hold values from -6 to 6
- filters: bfloat16 [512, 128], P(('ch', 'sub')), may hold values from -0.5 to 0.5
- skip_gain: float32 [8192], P(('ch', 'sub')), may hold values from 0.5 to 1.5
- attn_query: bfloat16 [3072, 8192], P(('rep', 'ctx'), ('ch', 'sub')), parts along dimension 0, may hold values from -40 to 40
- attn_key: bfloat16 [3072, 8192], P(('rep', 'ctx'), ('ch', 'sub')), parts along dimension 0, may hold values from -5 to 5
- genome_starts: int32 [8], P('rep'), parts along dimension 0, may hold values from 0 to 1408, as said below
Outputs:
- hyena_mix: bfloat16 [3072, 8192], P(('rep', 'ctx'), ('ch', 'sub')), parts along dimension 0
- attended: bfloat16 [3072, 8192], P(('rep', 'ctx'), ('ch', 'sub')), parts along dimension 0
There are 2 independent parts, one for each index of `rep`. A program takes and returns all parts, laid end to end along the dimension named above; an argument that names none is the same for every part. Nothing has to cross between parts.
Inputs may be any that keep to these rules, and one draw needn't show every extreme that they name: genome_starts[0] is 0; the entries rise, each by 128 or more, and the last genome holds exactly 128 positions.
All inputs are finite; a program needn't handle non-finite values.
Results may differ from a plain program's by a relative error of at most 0.0059.
Values may be sent and summed in bfloat16 or wider, within the bound.
A program may use at most 128 MiB of HBM per device.

v0:
```python
from functools import partial
import math

import jax
import jax.numpy as jnp
from jax import lax
from jax.sharding import PartitionSpec as P

HEAD_DIM = 128


def passed_along(value, axis, by):
    devices = lax.axis_size(axis)
    pairs = [(i, i + by) for i in range(devices) if 0 <= i + by < devices]
    return lax.ppermute(value, axis, pairs)


def genome_index(positions, genome_starts):
    inside = genome_starts[None, :] <= positions[:, None]
    return jnp.sum(inside.astype(jnp.int32), axis=1) - 1


def genome_begin(positions, genome_starts):
    inside = genome_starts[None, :] <= positions[:, None]
    return jnp.max(jnp.where(inside, genome_starts[None, :], 0), axis=1)


def grouped_filter(product, parity, filters, left_pad):
    channels = product.shape[1]
    group_width = channels // filters.shape[0]
    kernel = jnp.repeat(filters, group_width, axis=0).T[::-1][:, None, :]
    nothing = jnp.zeros_like(product)
    even_rows = jnp.where((parity == 0)[:, None], product, nothing)
    odd_rows = jnp.where((parity == 1)[:, None], product, nothing)
    stacked = jnp.stack([even_rows, odd_rows])
    return lax.conv_general_dilated(
        stacked,
        kernel,
        (1,),
        [(left_pad, 0)],
        dimension_numbers=("NWC", "WIO", "NWC"),
        feature_group_count=channels,
        preferred_element_type=jnp.float32,
    )


def attend_update(carried, queries, query_pos, query_begin, key_heads, value_heads, key_pos):
    weighted, running_max, weight_sum = carried
    score_scale = 1.0 / math.sqrt(HEAD_DIM)
    scores = (
        jnp.einsum("qhd,khd->hqk", queries, key_heads, preferred_element_type=jnp.float32)
        * score_scale
    )
    visible = (key_pos[None, :] <= query_pos[:, None]) & (key_pos[None, :] >= query_begin[:, None])
    new_max = jnp.maximum(running_max, jnp.max(jnp.where(visible[None], scores, -1e30), axis=2))
    weights = jnp.exp(jnp.where(visible[None], scores - new_max[:, :, None], -1e30))
    mixed = jnp.einsum(
        "hqk,khd->hqd",
        weights.astype(jnp.bfloat16),
        value_heads,
        preferred_element_type=jnp.float32,
    )
    return (mixed, new_max, jnp.sum(weights, axis=2))


def keep_state(carried):
    return carried


def per_device(
    hyena_query, hyena_key, hyena_value, filters, skip_gain, attn_query, attn_key, genome_starts
):
    local_rows, channels = hyena_key.shape
    taps = filters.shape[1]
    shard_first = lax.axis_index("ctx") * local_rows
    product = lax.optimization_barrier(
        (hyena_key.astype(jnp.float32) * hyena_value.astype(jnp.float32)).astype(jnp.bfloat16)
    )
    earlier = passed_along(product[local_rows - (taps - 1) :], "ctx", 1)
    extended = jnp.concatenate([earlier, product], axis=0)
    extended_pos = shard_first - (taps - 1) + jnp.arange(local_rows + taps - 1, dtype=jnp.int32)
    both_parities = grouped_filter(
        extended, genome_index(extended_pos, genome_starts) % 2, filters, 0
    )
    own_pos = shard_first + jnp.arange(local_rows, dtype=jnp.int32)
    own_parity = genome_index(own_pos, genome_starts) % 2
    filtered = jnp.where((own_parity == 0)[:, None], both_parities[0], both_parities[1])
    hyena_mix = (
        hyena_query.astype(jnp.float32)
        * (filtered + skip_gain[None, :] * product.astype(jnp.float32))
    ).astype(jnp.bfloat16)
    head_count = channels // HEAD_DIM
    queries = attn_query.reshape(local_rows, head_count, HEAD_DIM)
    pairs = [(queries, own_pos)]
    groups = [
        (group_queries, group_pos, genome_begin(group_pos, genome_starts))
        for group_queries, group_pos in pairs
    ]
    initial = tuple(
        (
            (
                jnp.zeros((head_count, group_pos.shape[0], HEAD_DIM), jnp.float32),
                jnp.full((head_count, group_pos.shape[0]), -1e30, jnp.float32),
                jnp.zeros((head_count, group_pos.shape[0]), jnp.float32),
            )
            for group_queries, group_pos, group_begin in groups
        )
    )
    offset_row = jnp.int32(0)
    keys_piece = lax.all_gather(attn_key, "ctx", axis=0, tiled=True)
    values_piece = lax.all_gather(hyena_mix, "ctx", axis=0, tiled=True)
    key_rows = keys_piece.shape[0]
    key_heads = keys_piece.reshape(key_rows, head_count, HEAD_DIM)
    value_heads = values_piece.reshape(key_rows, head_count, HEAD_DIM)
    key_pos = jnp.arange(key_rows, dtype=jnp.int32)
    updated = []
    for state_now, (group_queries, group_pos, group_begin) in zip(initial, groups):
        needed = (offset_row <= jnp.max(group_pos)) & (offset_row + key_rows > jnp.min(group_begin))
        update = partial(
            attend_update,
            queries=group_queries,
            query_pos=group_pos,
            query_begin=group_begin,
            key_heads=key_heads,
            value_heads=value_heads,
            key_pos=key_pos,
        )
        updated.append(lax.cond(needed, update, keep_state, state_now))
    results = tuple(updated)
    outputs = []
    for weighted, running_max, weight_sum in results:
        finished = (weighted / weight_sum[:, :, None]).astype(jnp.bfloat16)
        outputs.append(finished.transpose(1, 0, 2).reshape(weighted.shape[1], channels))
    attended = outputs[0]
    return (hyena_mix, attended)


def solution(mesh):
    return jax.shard_map(
        per_device,
        mesh=mesh,
        in_specs=(
            P(("rep", "ctx"), ("ch", "sub")),
            P(("rep", "ctx"), ("ch", "sub")),
            P(("rep", "ctx"), ("ch", "sub")),
            P(("ch", "sub"), None),
            P(("ch", "sub")),
            P(("rep", "ctx"), ("ch", "sub")),
            P(("rep", "ctx"), ("ch", "sub")),
            P("rep"),
        ),
        out_specs=(P(("rep", "ctx"), ("ch", "sub")), P(("rep", "ctx"), ("ch", "sub"))),
        check_vma=False,
    )
```

profile of v0, /device:TPU:30, one launch (start us, length us, event | category | flops | bytes accessed | tf_op | source)
XLA Modules:
  0.0 355.2 jit_solution(4277070580375410780)
XLA Ops:
  7.2 0.0 copy-start.11
  7.2 0.0 copy-start.5
  7.2 0.0 all-gather.3.cloned.1.call-start
  7.2 0.7 all-gather.3.cloned.1.call-update
  7.9 0.0 all-gather.5.cloned.1.call-start
  8.0 2.5 multiply_convert_fusion
  10.5 0.0 copy-start
  10.5 1.0 slice.12
  11.5 1.3 collective-permute-start
  12.8 0.0 copy-start.6
  12.8 0.0 copy-done.11
  12.8 0.1 convert_reduce_fusion
  12.9 0.0 copy-done.5
  12.9 0.1 broadcast_in_dim.88
  13.0 1.5 rev.3
  14.5 0.9 copy.43
  15.5 0.7 fusion.24
  16.1 0.5 fusion.26
  16.7 22.7 %collective-permute-done = bf16[127,2048]{1,0:T(8,128)(2,1)} collective-permute-done((bf16[127,2048]{1,0:T(8,128)(2,1)}, bf16[127,2048]{1,0:T(8,128)(2,1)}, u32[]{:S(2)}, u32[]{:S(2)}) %collective-permute-start) | collective-permute-done | bytes 520224 | tf_op jit(solution)/shard_map/ppermute | solution.py:15
  39.4 1.8 copy_dynamic-update-slice_fusion.1
  41.2 2.6 copy_dynamic-update-slice_fusion
  43.8 0.0 copy-done
  43.8 0.0 copy-done.6
  43.8 8.6 %broadcast_select_fusion.1 = (bf16[1,511,2048]{2,0,1:T(2,128)(2,1)S(1)}, bf16[1,511,2048]{2,0,1:T(2,128)(2,1)S(1)}) fusion(bf16[1,511,2048]{2,0,1:T(2,128)(2,1)S(1)} %copy_dynamic-update-slice_fusion, pred[511]{0:T(512)(128)(4,1)S(1)} %get-tuple-element.33, pred[511]{0:T(512)(128)(4,1)S(1)} %broadcast_compare_fusion), kind=kLoop, calls=%fused_computation.18 | loop fusion | flops 2093056 | bytes 6280190 | tf_op jit(solution)/shard_map/jit(_where)/select_n | solution.py:33
  52.5 9.6 %fusion.39 = bf16[2,511,2048]{2,0,1:T(2,128)(2,1)S(1)} fusion(bf16[1,511,2048]{2,0,1:T(2,128)(2,1)S(1)} %get-tuple-element.40, bf16[1,511,2048]{2,0,1:T(2,128)(2,1)S(1)} %get-tuple-element.39), kind=kLoop, calls=%fused_computation.20.clone.1 | loop fusion | flops 8372224 | bytes 8372224 | tf_op jit(solution)/shard_map/conv_general_dilated | solution.py:36
  62.1 90.8 %fusion.14 = f32[2,384,2048]{2,0,1:T(2,128)} fusion(bf16[128,1,2048]{2,1,0:T(2,128)(2,1)S(1)} %copy.43, bf16[2,511,2048]{2,0,1:T(2,128)(2,1)S(1)} %fusion.39), kind=kOutput, calls=%fused_computation.19 | convolution fusion | flops 402653184 | bytes 11001856 | tf_op jit(solution)/shard_map/conv_general_dilated | solution.py:36
  153.0 0.0 copy-start.10
  153.0 13.9 %fusion.30 = (f32[1,384,2048]{2,0,1:T(1,128)}, f32[1,384,2048]{2,0,1:T(1,128)}) fusion(f32[2,384,2048]{2,0,1:T(2,128)} %fusion.14), kind=kLoop, calls=%fused_computation.54 | loop fusion | bytes 12582912 | tf_op jit(solution)/shard_map/slice | solution.py:87
  166.9 0.0 copy-done.1
  166.9 0.0 copy-done.4
  166.9 0.0 copy-done.9
  166.9 0.0 copy-done.10
  166.9 0.0 copy-start.8
  166.9 6.9 %fusion.21 = bf16[384,2048]{1,0:T(8,128)(2,1)} fusion(f32[1,384,2048]{2,0,1:T(1,128)} %get-tuple-element.38, f32[1,384,2048]{2,0,1:T(1,128)} %get-tuple-element.37, bf16[384,2048]{1,0:T(8,128)(2,1)S(1)} %copy-done.1, bf16[384,2048]{1,0:T(8,128)(2,1)S(1)} %copy-done.4, f32[2048]{0:T(1024)S(1)} %copy-done.9, pred[384]{0:T(512)(128)(4,1)S(1)} %copy-done.10), kind=kLoop, calls=%fused_computation.27 | loop fusion | flops 5505024 | bytes 11018624 | tf_op jit(solution)/shard_map/convert_element_type | solution.py:91
  173.8 0.0 all-gather.5.cloned.1.call-update
  173.8 0.6 fusion.28
  175.1 0.0 copy-done.8
  175.1 0.6 reduce_min.9
  176.4 0.0 all-gather.3.cloned.1.call-done
  176.5 112.9 %all-gather.5.cloned.1.call-done = bf16[1536,2048]{1,0:T(8,128)(2,1)} async-done(((bf16[384,2048]{1,0:T(8,128)(2,1)}), bf16[1536,2048]{1,0:T(8,128)(2,1)}) %all-gather.5.cloned.1.call-update) | async-done | bytes 6291472 | tf_op jit(solution)/shard_map/all_gather | solution.py:111
  289.3 57.2 %conditional.1 = (f32[16,384,128]{2,1,0:T(8,128)S(1)}, f32[16,384]{1,0:T(8,128)S(1)}) conditional(s32[]{:T(128)} %convert_element_type.41, () %tuple.16, (s32[1536]{0:T(1024)S(1)}, s32[1536]{0:T(1024)S(1)}, s32[384]{0:T(512)S(1)}, s32[384]{0:T(512)S(1)}, bf16[384,2048]{1,0:T(8,128)(2,1)}, /*index=5*/bf16[1536,2048]{1,0:T(8,128)(2,1)}, ...), branch_computations={%region_5.6_spmd, %region_6.9_spmd} | conditional | flops 4937410560 | bytes 137788496 | solution.py:128
  289.3 0.5 compare_and_fusion
  289.9 0.0 copy-start.2
  289.9 18.5 %select_reduce_fusion = (f32[16,384]{1,0:T(8,128)S(1)}, f32[16,384,1536]{2,1,0:T(8,128)}) fusion(pred[384,1536]{1,0:T(8,128)(4,1)S(1)} %compare_and_fusion, bf16[1536,2048]{1,0:T(8,128)(2,1)} %get-tuple-element.21, bf16[384,2048]{1,0:T(8,128)(2,1)} %get-tuple-element.30), kind=kOutput, calls=%fused_computation.1 | convolution fusion | flops 2444224512 | bytes 46227456 | tf_op jit(solution)/shard_map/cond/branch_1_fun/qhd,khd->hqk/dot_general | solution.py:51
  308.4 0.0 copy-start.3
  308.4 21.0 %fusion.2 = f32[16,384,128]{2,1,0:T(8,128)S(1)} fusion(f32[16,384,1536]{2,1,0:T(8,128)} %get-tuple-element.36, f32[16,384]{1,0:T(8,128)S(1)} %broadcast_maximum_fusion, pred[384,1536]{1,0:T(8,128)(4,1)} %copy-done.2, bf16[1536,2048]{1,0:T(8,128)(2,1)} %get-tuple-element.22), kind=kOutput, calls=%fused_computation.4 | convolution fusion | flops 2453667840 | bytes 47800320 | tf_op jit(solution)/shard_map/cond/branch_1_fun/hqk,khd->hqd/dot_general | solution.py:57
  329.4 17.1 %fusion = f32[16,384]{1,0:T(8,128)S(1)} fusion(f32[16,384,1536]{2,1,0:T(8,128)} %get-tuple-element.36, f32[16,384]{1,0:T(8,128)S(1)} %broadcast_maximum_fusion, pred[384,1536]{1,0:T(8,128)(4,1)S(1)} %copy-done.3), kind=kLoop, calls=%fused_computation.2 | loop fusion | flops 37742592 | bytes 38387712 | tf_op jit(solution)/shard_map/cond/branch_1_fun/reduce_sum | solution.py:63
  346.5 1.9 copy_bitcast_fusion.1
  (13 shorter events, 0.0 us)
Async XLA Ops:
  7.2 5.7 %copy-start.11 = (s32[4]{0:T(128)S(1)}, s32[4]{0:T(128)}, u32[]{:S(2)}) copy-start(s32[4]{0:T(128)} %param.17) | copy-start | bytes 52
  7.2 5.8 %copy-start.5 = (bf16[128,128]{1,0:T(8,128)(2,1)S(1)}, bf16[128,128]{1,0:T(8,128)(2,1)}, u32[]{:S(2)}) copy-start(bf16[128,128]{1,0:T(8,128)(2,1)} %param.13) | copy-start | bytes 98308
  7.2 169.3 %all-gather.3.cloned.1.call-start = ((), (), s32[]{:S(2)}) async-start(), calls=%async_computation | async-start | bytes 7864320 | tf_op jit(solution)/shard_map/all_gather | solution.py:110
  7.9 281.4 %all-gather.5.cloned.1.call-start = ((), (), s32[]{:S(2)}) async-start(), calls=%async_computation.1 | async-start | bytes 7864320 | tf_op jit(solution)/shard_map/all_gather | solution.py:111
  10.5 33.4 %copy-start = (bf16[384,2048]{1,0:T(8,128)(2,1)}, bf16[384,2048]{1,0:T(8,128)(2,1)S(1)}, u32[]{:S(2)}) copy-start(bf16[384,2048]{1,0:T(8,128)(2,1)S(1)} %multiply_convert_fusion) | copy-start | bytes 4718596
  11.5 27.9 %collective-permute-start = (bf16[127,2048]{1,0:T(8,128)(2,1)}, bf16[127,2048]{1,0:T(8,128)(2,1)}, u32[]{:S(2)}, u32[]{:S(2)}) collective-permute-start(bf16[127,2048]{1,0:T(8,128)(2,1)} %slice.12), channel_id=1, source_target_pairs={{0,4},{4,8},{8,12},{1,5},{5,9},{9,13},{2,6},{6,10},{10,14},{3,7},{... | collective-permute-start | bytes 1560584 | tf_op jit(solution)/shard_map/ppermute | solution.py:15
  12.8 31.0 %copy-start.6 = (s32[384]{0:T(512)}, s32[384]{0:T(512)S(1)}, u32[]{:S(2)}) copy-start(s32[384]{0:T(512)S(1)} %iota_add_fusion.1) | copy-start | bytes 4612
  153.0 13.9 %copy-start.1 = (bf16[384,2048]{1,0:T(8,128)(2,1)S(1)}, bf16[384,2048]{1,0:T(8,128)(2,1)}, u32[]{:S(2)}) copy-start(bf16[384,2048]{1,0:T(8,128)(2,1)} %copy-done) | copy-start | bytes 4718596
  153.0 13.9 %copy-start.4 = (bf16[384,2048]{1,0:T(8,128)(2,1)S(1)}, bf16[384,2048]{1,0:T(8,128)(2,1)}, u32[]{:S(2)}) copy-start(bf16[384,2048]{1,0:T(8,128)(2,1)} %param.10) | copy-start | bytes 4718596
  153.0 13.9 %copy-start.9 = (f32[2048]{0:T(1024)S(1)}, f32[2048]{0:T(1024)}, u32[]{:S(2)}) copy-start(f32[2048]{0:T(1024)} %param.14) | copy-start | bytes 24580
  153.0 13.9 %copy-start.10 = (pred[384]{0:T(512)(128)(4,1)S(1)}, pred[384]{0:T(512)(128)(4,1)}, u32[]{:S(2)}) copy-start(pred[384]{0:T(512)(128)(4,1)} %fusion.26) | copy-start | bytes 1156
  166.9 8.2 %copy-start.8 = (s32[384]{0:T(512)S(1)}, s32[384]{0:T(512)}, u32[]{:S(2)}) copy-start(s32[384]{0:T(512)} %get-tuple-element.31) | copy-start | bytes 4612
  166.9 122.4 %copy-start.7 = (s32[384]{0:T(512)S(1)}, s32[384]{0:T(512)}, u32[]{:S(2)}) copy-start(s32[384]{0:T(512)} %copy-done.6) | copy-start | bytes 4612
  289.9 18.5 %copy-start.2 = (pred[384,1536]{1,0:T(8,128)(4,1)}, pred[384,1536]{1,0:T(8,128)(4,1)S(1)}, u32[]{:S(2)}) copy-start(pred[384,1536]{1,0:T(8,128)(4,1)S(1)} %compare_and_fusion) | copy-start | bytes 1769476 | tf_op jit(solution)/shard_map/cond
  308.4 21.0 %copy-start.3 = (pred[384,1536]{1,0:T(8,128)(4,1)S(1)}, pred[384,1536]{1,0:T(8,128)(4,1)}, u32[]{:S(2)}) copy-start(pred[384,1536]{1,0:T(8,128)(4,1)} %copy-done.2) | copy-start | bytes 1769476 | tf_op jit(solution)/shard_map/cond
Sparse Core Ops, SparseCore 0:
  9.6 119.3 all-gather.2
  174.0 115.3 all-gather.4
where the time goes:
time: 360 us; the launch traced here: 355 us
  waiting for transfers between devices  136 us (38%)
  matrix products  130 us (36%)
  other arithmetic  49.8 us (14%)
  local copies, waits for them, and re-layouts  21.9 us (6%)
  between operations  15.6 us (4%)
    all_gather x1, waiting for transfers between devices, per_device(): values_piece = lax.all_gather(hyena_mix, 'ctx', axis=0, tiled=True)  113 us
    conv_general_dilated x1, matrix products, grouped_filter(): lax.conv_general_dilated(stacked, kernel, (1,), [(left_pad, 0)], dimensio...  90.8 us
    ppermute x1, waiting for transfers between devices, passed_along(): return lax.ppermute(value, axis, pairs)  22.7 us
    dot_general x1, matrix products, attend_update(): jnp.einsum('hqk,khd->hqd', weights.astype(jnp.bfloat16), value_heads, pre...  21 us
    dot_general x1, matrix products, attend_update(): jnp.einsum('qhd,khd->hqk', queries, key_heads, preferred_element_type=jnp...  18.5 us
    reduce_sum x1, other arithmetic, attend_update(): return (mixed, new_max, jnp.sum(weights, axis=2))  17.1 us
    slice x1, local copies, waits for them, and re-layouts, per_device(): both_parities[1]  13.9 us
    conv_general_dilated x1, other arithmetic, grouped_filter(): lax.conv_general_dilated(stacked, kernel, (1,), [(left_pad, 0)], dimensio...  9.64 us
  transfers between devices with their start and end apart: 3, of which 2 were waited for; matrix products, arithmetic and copies ran while one was open for 40% of the time, Pallas kernels for 0%

commit v1 on v0

--- a/solution.py
+++ b/solution.py
@@ -4,6 +4,8 @@
 import jax
 import jax.numpy as jnp
 from jax import lax
+from jax.experimental import pallas as pl
+from jax.experimental.pallas import tpu as pltpu
 from jax.sharding import PartitionSpec as P
 
 HEAD_DIM = 128
@@ -67,7 +69,7 @@
     return carried
 
 
-def per_device(
+def gathered_plan(
     hyena_query, hyena_key, hyena_value, filters, skip_gain, attn_query, attn_key, genome_starts
 ):
     local_rows, channels = hyena_key.shape
@@ -135,9 +137,321 @@
     return (hyena_mix, attended)
 
 
+NEVER = -1e29
+BLOCK = 128
+CHUNKS = 4
+EXPONENT = math.log2(math.e) / math.sqrt(HEAD_DIM)
+
+
+def begin_of(positions, facts_ref, genomes):
+    begin = jnp.zeros_like(positions)
+    for genome in range(genomes):
+        start = facts_ref[genome]
+        begin = jnp.where(start <= positions, jnp.maximum(begin, start), begin)
+    return begin
+
+
+def hyena_kernel(genomes, facts_ref, query_ref, key_ref, value_ref, halo_ref, taps_ref, gain_ref,
+                 mix_ref, extended, masks):
+    rows = key_ref.shape[0]
+    blocks = rows // BLOCK
+    groups = taps_ref.shape[0]
+    group_width = BLOCK // groups
+
+    @pl.when(pl.program_id(0) == 0)
+    def _():
+        first = facts_ref[genomes] * rows
+        for b in range(blocks):
+            i = lax.broadcasted_iota(jnp.int32, (BLOCK, 2 * BLOCK), 0)
+            j = lax.broadcasted_iota(jnp.int32, (BLOCK, 2 * BLOCK), 1) - BLOCK
+            begin = begin_of(i + (first + b * BLOCK), facts_ref, genomes)
+            tap = i - j
+            inside = (tap >= 0) & (tap < BLOCK) & (j + (first + b * BLOCK) >= begin)
+            masks[b] = jnp.where(inside, 1.0, 0.0).astype(jnp.bfloat16)
+
+    product = (key_ref[...].astype(jnp.float32) * value_ref[...].astype(jnp.float32)).astype(
+        jnp.bfloat16
+    )
+    extended[:BLOCK] = halo_ref[...]
+    extended[BLOCK:] = product
+    lane_group = lax.broadcasted_iota(jnp.int32, (BLOCK, BLOCK), 1) // group_width
+    totals = [jnp.zeros((BLOCK, BLOCK), jnp.float32) for b in range(blocks)]
+    for g in range(groups):
+        row = jnp.broadcast_to(taps_ref[g : g + 1, :], (BLOCK, BLOCK))
+        turned = pltpu.roll(row, 0, 1, stride=1, stride_axis=0).astype(jnp.bfloat16)
+        both = jnp.concatenate([turned, turned], axis=1)
+        for b in range(blocks):
+            band = both * masks[b]
+            part = jnp.dot(
+                band, extended[b * BLOCK : (b + 2) * BLOCK], preferred_element_type=jnp.float32
+            )
+            totals[b] = jnp.where(lane_group == g, part, totals[b])
+    for b in range(blocks):
+        here = slice(b * BLOCK, (b + 1) * BLOCK)
+        wide = extended[(b + 1) * BLOCK : (b + 2) * BLOCK].astype(jnp.float32)
+        mix_ref[here] = (
+            query_ref[here].astype(jnp.float32) * (totals[b] + gain_ref[...] * wide)
+        ).astype(jnp.bfloat16)
+
+
+def hyena(facts, genomes, query, key, value, halo, turned_taps, skip_gain):
+    rows, channels = key.shape
+    groups = turned_taps.shape[0] * BLOCK // channels
+    column = lambda c, facts_ref: (0, c)
+    return pl.pallas_call(
+        partial(hyena_kernel, genomes),
+        out_shape=jax.ShapeDtypeStruct((rows, channels), jnp.bfloat16),
+        grid_spec=pltpu.PrefetchScalarGridSpec(
+            num_scalar_prefetch=1,
+            grid=(channels // BLOCK,),
+            in_specs=[
+                pl.BlockSpec((rows, BLOCK), column),
+                pl.BlockSpec((rows, BLOCK), column),
+                pl.BlockSpec((rows, BLOCK), column),
+                pl.BlockSpec((BLOCK, BLOCK), column),
+                pl.BlockSpec((groups, BLOCK), lambda c, facts_ref: (c, 0)),
+                pl.BlockSpec((1, BLOCK), column),
+            ],
+            out_specs=pl.BlockSpec((rows, BLOCK), column),
+            scratch_shapes=[
+                pltpu.VMEM((rows + BLOCK, BLOCK), jnp.bfloat16),
+                pltpu.VMEM((rows // BLOCK, BLOCK, 2 * BLOCK), jnp.bfloat16),
+            ],
+        ),
+        cost_estimate=pl.CostEstimate(
+            flops=rows * channels * 2 * 2 * BLOCK * groups,
+            bytes_accessed=rows * channels * 8,
+            transcendentals=0,
+        ),
+        name="hyena",
+    )(facts, query, key, value, halo, turned_taps, skip_gain)
+
+
+def attend_tile(queries, keys, values, query_first, key_first, facts_ref, genomes, carried):
+    scores = lax.dot_general(
+        queries, keys, (((1,), (1,)), ((), ())), preferred_element_type=jnp.float32
+    )
+    query_pos = query_first + lax.broadcasted_iota(jnp.int32, (queries.shape[0], 1), 0)
+    begin = begin_of(query_pos, facts_ref, genomes)
+    key_pos = key_first + lax.broadcasted_iota(jnp.int32, scores.shape, 1)
+    visible = (key_pos >= begin) & (key_pos <= query_pos)
+    scores = jnp.where(visible, scores, 10 * NEVER)
+    highest, total, mixed = carried
+    new_highest = jnp.maximum(highest, jnp.max(scores, axis=1, keepdims=True))
+    weights = jnp.exp2((scores - new_highest) * EXPONENT)
+    fade = jnp.exp2((highest - new_highest) * EXPONENT)
+    new_mixed = fade * mixed + jnp.dot(
+        weights.astype(jnp.bfloat16), values, preferred_element_type=jnp.float32
+    )
+    return new_highest, fade * total + jnp.sum(weights, axis=1, keepdims=True), new_mixed
+
+
+def attend_kernel(genomes, facts_ref, own_q, next_q, last_q, own_k, own_v, far_k, far_v,
+                  own_o, next_o, last_o, own_l, next_l, last_l, high, total, mixed):
+    rows = own_q.shape[0]
+    head = pl.program_id(0)
+    shard = facts_ref[genomes]
+    own_first = shard * rows
+
+    def update(here, queries, keys, values, query_first, key_first):
+        carried = (high[here], total[here], mixed[here])
+        high[here], total[here], mixed[here] = attend_tile(
+            queries, keys, values, query_first, key_first, facts_ref, genomes, carried
+        )
+
+    def clear():
+        high[...] = jnp.full_like(high, NEVER)
+        total[...] = jnp.zeros_like(total)
+        mixed[...] = jnp.zeros_like(mixed)
+
+    def finish(out_ref, log_ref):
+        summed = total[...]
+        some = summed > 0
+        safe = jnp.where(some, summed, 1.0)
+        out_ref[...] = (mixed[...] / safe).astype(out_ref.dtype)
+        log = jnp.where(some, high[...] * EXPONENT + jnp.log2(safe), NEVER)
+        log_ref[pl.ds(head, 1), :] = jnp.transpose(jnp.broadcast_to(log, (rows, BLOCK)))[:1]
+
+    everything = slice(0, rows)
+
+    def reach(query_first):
+        begin = jnp.int32(0)
+        for genome in range(genomes):
+            start = facts_ref[genome]
+            begin = jnp.where(start <= query_first, jnp.maximum(begin, start), begin)
+        return begin
+
+    clear()
+
+    @pl.when((shard == 1) & (reach(own_first) < rows))
+    def _():
+        update(everything, own_q[...], far_k[...], far_v[...], own_first, 0)
+
+    for b in range(rows // BLOCK):
+        here = slice(b * BLOCK, (b + 1) * BLOCK)
+        upto = slice(0, (b + 1) * BLOCK)
+        update(here, own_q[here], own_k[upto], own_v[upto], own_first + b * BLOCK, own_first)
+    finish(own_o, own_l)
+
+    for queries, query_shard, used, out_ref, log_ref in (
+        (next_q, shard + 1, (shard == 1) | (shard == 2), next_o, next_l),
+        (last_q, 3, shard == 1, last_o, last_l),
+    ):
+        query_first = query_shard * rows
+        begin = reach(query_first)
+        needed = used & (begin < own_first + rows)
+
+        @pl.when(needed)
+        def _():
+            clear()
+            update(everything, queries[...], own_k[...], own_v[...], query_first, own_first)
+
+            @pl.when((shard == 1) & (begin < rows))
+            def _():
+                update(everything, queries[...], far_k[...], far_v[...], query_first, 0)
+
+            finish(out_ref, log_ref)
+
+        @pl.when(jnp.logical_not(needed))
+        def _():
+            out_ref[...] = jnp.zeros_like(out_ref)
+            log_ref[pl.ds(head, 1), :] = jnp.full((1, rows), NEVER, jnp.float32)
+
+
+def attend(facts, genomes, chunk, heads, own_q, next_q, last_q, own_k, own_v, far_k, far_v):
+    rows = own_q.shape[0]
+    whole = pl.BlockSpec((rows, HEAD_DIM), lambda h, facts_ref: (0, chunk * heads + h))
+    piece = pl.BlockSpec((rows, HEAD_DIM), lambda h, facts_ref: (0, h))
+    logs = pl.BlockSpec((heads, rows), lambda h, facts_ref: (0, 0))
+    width = heads * HEAD_DIM
+    return pl.pallas_call(
+        partial(attend_kernel, genomes),
+        out_shape=(
+            jax.ShapeDtypeStruct((rows, width), jnp.float32),
+            jax.ShapeDtypeStruct((rows, width), jnp.bfloat16),
+            jax.ShapeDtypeStruct((rows, width), jnp.bfloat16),
+            jax.ShapeDtypeStruct((heads, rows), jnp.float32),
+            jax.ShapeDtypeStruct((heads, rows), jnp.float32),
+            jax.ShapeDtypeStruct((heads, rows), jnp.float32),
+        ),
+        grid_spec=pltpu.PrefetchScalarGridSpec(
+            num_scalar_prefetch=1,
+            grid=(heads,),
+            in_specs=[whole, piece, piece, whole, whole, piece, piece],
+            out_specs=[piece, piece, piece, logs, logs, logs],
+            scratch_shapes=[
+                pltpu.VMEM((rows, 1), jnp.float32),
+                pltpu.VMEM((rows, 1), jnp.float32),
+                pltpu.VMEM((rows, HEAD_DIM), jnp.float32),
+            ],
+        ),
+        compiler_params=pltpu.CompilerParams(vmem_limit_bytes=32 << 20),
+        cost_estimate=pl.CostEstimate(
+            flops=24 * rows * rows * width,
+            bytes_accessed=rows * width * 22,
+            transcendentals=6 * rows * rows * heads,
+        ),
+        name="attend",
+    )(facts, own_q, next_q, last_q, own_k, own_v, far_k, far_v)
+
+
+def combine_kernel(genomes, facts_ref, *refs):
+    own_o, near_o, far_o, own_l, near_l, far_l = refs[-7:-1]
+    out_ref = refs[-1]
+    rows = own_o.shape[0]
+    head = pl.program_id(0)
+    shard = facts_ref[genomes]
+
+    def column(log_ref):
+        return jnp.transpose(jnp.broadcast_to(log_ref[pl.ds(head, 1), :], (BLOCK, rows)))
+
+    own = column(own_l)
+    near = jnp.where(shard >= 2, column(near_l), NEVER)
+    far = jnp.where(shard == 3, column(far_l), NEVER)
+    highest = jnp.maximum(own, jnp.maximum(near, far))
+    own, near, far = jnp.exp2(own - highest), jnp.exp2(near - highest), jnp.exp2(far - highest)
+    mixed = (
+        own * own_o[...]
+        + near * near_o[...].astype(jnp.float32)
+        + far * far_o[...].astype(jnp.float32)
+    )
+    out_ref[...] = (mixed / (own + near + far)).astype(out_ref.dtype)
+
+
+def combine(facts, genomes, chunk, heads, channels, earlier, *pieces):
+    rows = pieces[0].shape[0]
+    piece = pl.BlockSpec((rows, HEAD_DIM), lambda h, facts_ref: (0, h))
+    logs = pl.BlockSpec((heads, rows), lambda h, facts_ref: (0, 0))
+    held = () if earlier is None else (earlier,)
+    return pl.pallas_call(
+        partial(combine_kernel, genomes),
+        out_shape=jax.ShapeDtypeStruct((rows, channels), jnp.bfloat16),
+        grid_spec=pltpu.PrefetchScalarGridSpec(
+            num_scalar_prefetch=1,
+            grid=(heads,),
+            in_specs=[pl.BlockSpec(memory_space=pl.ANY)] * len(held) + [piece] * 3 + [logs] * 3,
+            out_specs=pl.BlockSpec(
+                (rows, HEAD_DIM), lambda h, facts_ref: (0, chunk * heads + h)
+            ),
+        ),
+        input_output_aliases={1: 0} if held else {},
+        cost_estimate=pl.CostEstimate(
+            flops=rows * heads * HEAD_DIM * 16,
+            bytes_accessed=rows * heads * HEAD_DIM * 10,
+            transcendentals=0,
+        ),
+        name="combine",
+    )(facts, *held, *pieces)
+
+
+def balanced_plan(
+    hyena_query, hyena_key, hyena_value, filters, skip_gain, attn_query, attn_key, genome_starts
+):
+    rows, channels = hyena_key.shape
+    genomes = genome_starts.shape[0]
+    shard = lax.axis_index("ctx")
+    facts = jnp.concatenate([genome_starts, jnp.full((1,), shard, jnp.int32)])
+    tail = (
+        hyena_key[rows - BLOCK :].astype(jnp.float32)
+        * hyena_value[rows - BLOCK :].astype(jnp.float32)
+    ).astype(jnp.bfloat16)
+    halo = passed_along(tail, "ctx", 1)
+    turned_taps = jnp.roll(filters[:, ::-1], 1, axis=1).astype(jnp.float32)
+    mix = hyena(
+        facts, genomes, hyena_query, hyena_key, hyena_value, halo, turned_taps, skip_gain[None, :]
+    )
+    heads = channels // HEAD_DIM // CHUNKS
+    width = heads * HEAD_DIM
+    attended = None
+    parts = []
+    for chunk in range(CHUNKS):
+        here = slice(chunk * width, (chunk + 1) * width)
+        queries = attn_query[:, here]
+        far_k = lax.ppermute(attn_key[:, here], "ctx", [(0, 1)])
+        next_q = lax.ppermute(queries, "ctx", [(2, 1), (3, 2)])
+        last_q = lax.ppermute(queries, "ctx", [(3, 1)])
+        far_v = lax.ppermute(mix[:, here], "ctx", [(0, 1)])
+        own_o, next_o, last_o, own_l, next_l, last_l = attend(
+            facts, genomes, chunk, heads, attn_query, next_q, last_q, attn_key, mix, far_k, far_v
+        )
+        parts.append(
+            (
+                own_o,
+                lax.ppermute(next_o, "ctx", [(1, 2), (2, 3)]),
+                lax.ppermute(last_o, "ctx", [(1, 3)]),
+                own_l,
+                lax.ppermute(next_l, "ctx", [(1, 2), (2, 3)]),
+                lax.ppermute(last_l, "ctx", [(1, 3)]),
+            )
+        )
+    for chunk in range(CHUNKS):
+        attended = combine(facts, genomes, chunk, heads, channels, attended, *parts[chunk])
+    return (mix, attended)
+
+
 def solution(mesh):
     return jax.shard_map(
-        per_device,
+        balanced_plan if mesh.shape["ctx"] == 4 else gathered_plan,
         mesh=mesh,
         in_specs=(
             P(("rep", "ctx"), ("ch", "sub")),

time: 360 us -> 220 us (0.61)
  matrix products: 130 us -> 0 us
  Pallas kernels: 0 us -> 66.1 us
  waiting for transfers between devices: 136 us -> 81.1 us
  starting transfers between devices: 1.36 us -> 51.3 us
  other arithmetic: 49.8 us -> 4.36 us
  between operations: 15.6 us -> 1.26 us
  local copies, waits for them, and re-layouts: 21.9 us -> 12.4 us
    all_gather x2 -> x0, waiting for transfers between devices: 113 us -> none  [the longest x1 113 us: per_device(): values_piece = lax.all_gather(hyena_mix, 'ctx', axis=0, tiled=True)]
    conv_general_dilated x1 -> x0, matrix products: 90.8 us -> none  [grouped_filter(): lax.conv_general_dilated(stacked, kernel, (1,), [(left_pad, 0)], dimensio...]
    ppermute x0 -> x32, waiting for transfers between devices: none -> 81.1 us  [the longest x4 42.6 us: balanced_plan(): lax.ppermute(last_l, 'ctx', [(1, 3)])]
    pallas_call x0 -> x9, Pallas kernels: none -> 66.1 us  [the longest x4 31.2 us: attend(): pl.pallas_call(partial(attend_kernel, genomes), out_shape=(jax.ShapeDtype...]
    ppermute x0 -> x32, starting transfers between devices: none -> 49.9 us  [the longest x4 12 us: balanced_plan(): next_q = lax.ppermute(queries, 'ctx', [(2, 1), (3, 2)])]
    dot_general x2 -> x0, matrix products: 39.4 us -> none  [the longest x1 21 us: attend_update(): jnp.einsum('hqk,khd->hqd', weights.astype(jnp.bfloat16), value_heads, pre...]
    ppermute x1, waiting for transfers between devices: 22.7 us -> 0.01 us  [passed_along(): return lax.ppermute(value, axis, pairs)]
    reduce_sum x2 -> x0, other arithmetic: 17.2 us -> none  [the longest x1 17.1 us: attend_update(): return (mixed, new_max, jnp.sum(weights, axis=2))]
  transfers between devices with their start and end apart: 3 -> 33, of which waited for: 2 -> 10; matrix products, arithmetic and copies ran while one was open for 40% -> 4% of each run, Pallas kernels for 0% -> 28%
where the time goes in v1:
time: 220 us; the launch traced here: 216 us
  waiting for transfers between devices  81.1 us (37%)
  Pallas kernels  66.1 us (30%)
  starting transfers between devices  51.3 us (23%)
  local copies, waits for them, and re-layouts  12.4 us (6%)
  other arithmetic  4.36 us (2%)
    ppermute x4, waiting for transfers between devices, balanced_plan(): lax.ppermute(last_l, 'ctx', [(1, 3)])  42.6 us
    pallas_call x4, Pallas kernels, attend(): pl.pallas_call(partial(attend_kernel, genomes), out_shape=(jax.ShapeDtype...  31.2 us
    ppermute x4, waiting for transfers between devices, balanced_plan(): lax.ppermute(next_l, 'ctx', [(1, 2), (2, 3)])  23.1 us
    pallas_call x4, Pallas kernels, combine(): pl.pallas_call(partial(combine_kernel, genomes), out_shape=jax.ShapeDtype...  18.9 us
    pallas_call x1, Pallas kernels, hyena(): pl.pallas_call(partial(hyena_kernel, genomes), out_shape=jax.ShapeDtypeSt...  16 us
    ppermute x4, starting transfers between devices, balanced_plan(): next_q = lax.ppermute(queries, 'ctx', [(2, 1), (3, 2)])  12 us
    ppermute x4, starting transfers between devices, balanced_plan(): last_q = lax.ppermute(queries, 'ctx', [(3, 1)])  9.87 us
    ppermute x4, waiting for transfers between devices, balanced_plan(): last_q = lax.ppermute(queries, 'ctx', [(3, 1)])  7.8 us
  transfers between devices with their start and end apart: 33, of which 10 were waited for; matrix products, arithmetic and copies ran while one was open for 4% of the time, Pallas kernels for 28%

profile of v1, /device:TPU:30, one launch (start us, length us, event | category | flops | bytes accessed | tf_op | source)
XLA Modules:
  0.0 216.4 jit_solution(5994576101188208055)
XLA Ops:
  0.6 2.2 %multiply_convert_fusion = bf16[128,2048]{1,0:T(8,128)(2,1)} fusion(bf16[384,2048]{1,0:T(8,128)(2,1)} %value_ref.1, bf16[384,2048]{1,0:T(8,128)(2,1)} %key_ref.1), kind=kLoop, calls=%fused_computation | loop fusion | flops 1048576 | bytes 1572864 | tf_op jit(solution)/shard_map/convert_element_type | solution.py:417
  2.9 1.4 collective-permute-start
  5.5 5.4 %collective-permute-start.1 = (bf16[384,512]{1,0:T(8,128)(2,1)}, bf16[384,512]{1,0:T(8,128)(2,1)}, u32[]{:S(2)}, u32[]{:S(2)}) collective-permute-start(bf16[384,512]{1,0:T(8,128)(2,1)} %get-tuple-element.61), channel_id=1, source_target_pairs={{8,4},{12,8},{9,5},{13,9},{10,6},{14,10},{11,7},{15,11},{24,20},{2... | collective-permute-start | bytes 1179656 | tf_op jit(solution)/shard_map/ppermute | solution.py:431
  10.9 2.1 collective-permute-start.2
  14.1 1.4 collective-permute-start.3
  15.5 1.3 collective-permute-start.10
  16.9 1.5 slice.57
  18.3 1.4 slice.58
  19.8 1.5 maximum_convert_fusion.taps_ref
  21.9 3.3 %collective-permute-start.9 = (bf16[384,512]{1,0:T(8,128)(2,1)}, bf16[384,512]{1,0:T(8,128)(2,1)}, u32[]{:S(2)}, u32[]{:S(2)}) collective-permute-start(bf16[384,512]{1,0:T(8,128)(2,1)} %get-tuple-element.60), channel_id=1, source_target_pairs={{8,4},{12,8},{9,5},{13,9},{10,6},{14,10},{11,7},{15,11},{24,20},{2... | collective-permute-start | bytes 1179656 | tf_op jit(solution)/shard_map/ppermute | solution.py:431
  25.2 1.4 collective-permute-start.11
  26.6 16.0 %hyena.1.own_v = bf16[384,2048]{1,0:T(8,128)(2,1)} custom-call(s32[5]{0:T(128)} %pad_add_fusion.facts_ref, bf16[384,2048]{1,0:T(8,128)(2,1)} %query_ref.1, bf16[384,2048]{1,0:T(8,128)(2,1)} %key_ref.1, bf16[384,2048]{1,0:T(8,128)(2,1)} %value_ref.1, bf16[128,2048]{1,0:T(8,128)(2,1)} %collective-permute-done.halo_ref, ...), custom_call_target="tpu_custom_call" | custom-call | flops 3221225472 | bytes 6291456 | tf_op jit(solution)/shard_map/hyena/pallas_call | solution.py:201
  42.5 1.3 collective-permute-start.17
  43.9 1.3 collective-permute-start.18
  46.1 1.5 fusion
  47.5 2.0 collective-permute-start.25
  50.2 3.4 %collective-permute-done.17.next_q = bf16[384,512]{1,0:T(8,128)(2,1)S(1)} collective-permute-done((bf16[384,512]{1,0:T(8,128)(2,1)}, bf16[384,512]{1,0:T(8,128)(2,1)S(1)}, u32[]{:S(2)}, u32[]{:S(2)}) %collective-permute-start.17) | collective-permute-done | bytes 393248 | tf_op jit(solution)/shard_map/ppermute | solution.py:431
  54.4 7.8 %collective-permute-done.18.last_q = bf16[384,512]{1,0:T(8,128)(2,1)S(1)} collective-permute-done((bf16[384,512]{1,0:T(8,128)(2,1)}, bf16[384,512]{1,0:T(8,128)(2,1)S(1)}, u32[]{:S(2)}, u32[]{:S(2)}) %collective-permute-start.18) | collective-permute-done | bytes 393248 | tf_op jit(solution)/shard_map/ppermute | solution.py:432
  62.2 5.2 %collective-permute-start.26 = (bf16[384,512]{1,0:T(8,128)(2,1)S(1)}, bf16[384,512]{1,0:T(8,128)(2,1)S(1)}, u32[]{:S(2)}, u32[]{:S(2)}) collective-permute-start(bf16[384,512]{1,0:T(8,128)(2,1)S(1)} %copy-done.12), channel_id=1, source_target_pairs={{12,4},{13,5},{14,6},{15,7},{28,20},{29,21},{30,22},{31,23}} | collective-permute-start | bytes 1179656 | tf_op jit(solution)/shard_map/ppermute | solution.py:432
  68.1 2.4 %collective-permute-done.25.next_q = bf16[384,512]{1,0:T(8,128)(2,1)S(1)} collective-permute-done((bf16[384,512]{1,0:T(8,128)(2,1)S(1)}, bf16[384,512]{1,0:T(8,128)(2,1)S(1)}, u32[]{:S(2)}, u32[]{:S(2)}) %collective-permute-start.25) | collective-permute-done | bytes 393248 | tf_op jit(solution)/shard_map/ppermute | solution.py:431
  71.9 7.9 %attend.4 = (f32[384,512]{1,0:T(8,128)S(1)}, bf16[384,512]{1,0:T(8,128)(2,1)S(1)}, bf16[384,512]{1,0:T(8,128)(2,1)S(1)}, f32[4,384]{1,0:T(4,128)S(1)}, f32[4,384]{1,0:T(4,128)S(1)}, /*index=5*/f32[4,384]{1,0:T(4,128)S(1)}) custom-call(s32[5]{0:T(128)S(1)} %copy-done.7, bf16[384,2048]{1,0:T(8,128)(2,1)S(1)} %copy-done, ...), custom_call_target="tpu_custom_call" | custom-call | flops 1811939328 | bytes 4325376 | tf_op jit(solution)/shard_map/attend/pallas_call | solution.py:327
  81.3 1.5 collective-permute-start.5
  82.8 8.0 %attend.5 = (f32[384,512]{1,0:T(8,128)S(1)}, bf16[384,512]{1,0:T(8,128)(2,1)S(1)}, bf16[384,512]{1,0:T(8,128)(2,1)S(1)}, f32[4,384]{1,0:T(4,128)S(1)}, f32[4,384]{1,0:T(4,128)S(1)}, /*index=5*/f32[4,384]{1,0:T(4,128)S(1)}) custom-call(s32[5]{0:T(128)S(1)} %copy-done.7, bf16[384,2048]{1,0:T(8,128)(2,1)S(1)} %copy-done, ...), custom_call_target="tpu_custom_call" | custom-call | flops 1811939328 | bytes 4325376 | tf_op jit(solution)/shard_map/attend/pallas_call | solution.py:327
  91.4 1.3 collective-permute-start.6
  92.7 1.3 collective-permute-start.13
  94.0 1.3 collective-permute-start.7
  95.3 1.3 collective-permute-start.8
  96.6 16.1 %collective-permute-done.7.refs_4_ = f32[4,384]{1,0:T(4,128)S(1)} collective-permute-done((f32[4,384]{1,0:T(4,128)S(1)}, f32[4,384]{1,0:T(4,128)S(1)}, u32[]{:S(2)}, u32[]{:S(2)}) %collective-permute-start.7) | collective-permute-done | bytes 6176 | tf_op jit(solution)/shard_map/ppermute | solution.py:443
  112.7 1.3 collective-permute-start.15
  113.9 23.1 %collective-permute-done.8.refs_5_ = f32[4,384]{1,0:T(4,128)S(1)} collective-permute-done((f32[4,384]{1,0:T(4,128)S(1)}, f32[4,384]{1,0:T(4,128)S(1)}, u32[]{:S(2)}, u32[]{:S(2)}) %collective-permute-start.8) | collective-permute-done | bytes 6176 | tf_op jit(solution)/shard_map/ppermute | solution.py:444
  139.0 7.4 %attend.6 = (f32[384,512]{1,0:T(8,128)S(1)}, bf16[384,512]{1,0:T(8,128)(2,1)S(1)}, bf16[384,512]{1,0:T(8,128)(2,1)S(1)}, f32[4,384]{1,0:T(4,128)S(1)}, f32[4,384]{1,0:T(4,128)S(1)}, /*index=5*/f32[4,384]{1,0:T(4,128)S(1)}) custom-call(s32[5]{0:T(128)S(1)} %copy-done.7, bf16[384,2048]{1,0:T(8,128)(2,1)S(1)} %copy-done, ...), custom_call_target="tpu_custom_call" | custom-call | flops 1811939328 | bytes 4325376 | tf_op jit(solution)/shard_map/attend/pallas_call | solution.py:327
  147.0 1.3 collective-permute-start.23
  148.3 1.3 collective-permute-start.24
  149.6 6.7 %collective-permute-done.23.refs_5_ = f32[4,384]{1,0:T(4,128)S(1)} collective-permute-done((f32[4,384]{1,0:T(4,128)S(1)}, f32[4,384]{1,0:T(4,128)S(1)}, u32[]{:S(2)}, u32[]{:S(2)}) %collective-permute-start.23) | collective-permute-done | bytes 6176 | tf_op jit(solution)/shard_map/ppermute | solution.py:443
  156.2 1.3 collective-permute-start.14
  157.5 8.6 %collective-permute-done.24.refs_6_ = f32[4,384]{1,0:T(4,128)S(1)} collective-permute-done((f32[4,384]{1,0:T(4,128)S(1)}, f32[4,384]{1,0:T(4,128)S(1)}, u32[]{:S(2)}, u32[]{:S(2)}) %collective-permute-start.24) | collective-permute-done | bytes 6176 | tf_op jit(solution)/shard_map/ppermute | solution.py:444
  166.2 1.3 collective-permute-start.21
  167.5 1.5 collective-permute-start.22
  169.0 8.0 %attend.7 = (f32[384,512]{1,0:T(8,128)S(1)}, bf16[384,512]{1,0:T(8,128)(2,1)}, bf16[384,512]{1,0:T(8,128)(2,1)}, f32[4,384]{1,0:T(4,128)S(1)}, f32[4,384]{1,0:T(4,128)}, /*index=5*/f32[4,384]{1,0:T(4,128)S(1)}) custom-call(s32[5]{0:T(128)S(1)} %copy-done.7, bf16[384,2048]{1,0:T(8,128)(2,1)S(1)} %copy-done, ...), custom_call_target="tpu_custom_call" | custom-call | flops 1811939328 | bytes 4325376 | tf_op jit(solution)/shard_map/attend/pallas_call | solution.py:327
  178.5 1.3 collective-permute-start.29
  179.8 1.3 collective-permute-start.30
  181.1 1.3 collective-permute-start.31
  182.4 1.8 collective-permute-done.21.refs_2_
  185.5 4.7 %combine.4.refs_0_ = bf16[384,2048]{1,0:T(8,128)(2,1)} custom-call(s32[5]{0:T(128)} %pad_add_fusion.facts_ref, f32[384,512]{1,0:T(8,128)} %copy-done.6, bf16[384,512]{1,0:T(8,128)(2,1)} %copy-done.14, bf16[384,512]{1,0:T(8,128)(2,1)} %copy-done.15, f32[4,384]{1,0:T(4,128)} %copy-done.8, f32[4,384]{1,0:T(4,128)} %copy-done.21, f32[4,384]{1,0:T(4,128)} %copy-done.22), custom_call_target="tpu_custom_call" | custom-call | flops 3145728 | bytes 1966080 | tf_op jit(solution)/shard_map/combine/pallas_call | solution.py:386
  190.3 4.7 %combine.5.refs_0_ = bf16[384,2048]{1,0:T(8,128)(2,1)} custom-call(s32[5]{0:T(128)} %pad_add_fusion.facts_ref, bf16[384,2048]{1,0:T(8,128)(2,1)} %combine.4.refs_0_, f32[384,512]{1,0:T(8,128)} %copy-done.3, bf16[384,512]{1,0:T(8,128)(2,1)} %copy-done.16, bf16[384,512]{1,0:T(8,128)(2,1)} %copy-done.19, ...), custom_call_target="tpu_custom_call", output_to_operand_aliasing={{}: (1, {})} | custom-call | flops 3145728 | bytes 1966080 | tf_op jit(solution)/shard_map/combine/pallas_call | solution.py:386
  195.0 4.7 %combine.6.refs_0_ = bf16[384,2048]{1,0:T(8,128)(2,1)} custom-call(s32[5]{0:T(128)} %pad_add_fusion.facts_ref, bf16[384,2048]{1,0:T(8,128)(2,1)} %combine.5.refs_0_, f32[384,512]{1,0:T(8,128)} %copy-done.4, bf16[384,512]{1,0:T(8,128)(2,1)} %copy-done.17, bf16[384,512]{1,0:T(8,128)(2,1)} %collective-permute-done.22.refs_3_, ...), custom_call_target="tpu_custom_call", output_to_operand_aliasing={{}: (1, {})} | custom-call | flops 3145728 | bytes 1966080 | tf_op jit(solution)/shard_map/combine/pallas_call | solution.py:386
  200.0 10.8 %collective-permute-done.32.refs_6_ = f32[4,384]{1,0:T(4,128)S(1)} collective-permute-done((f32[4,384]{1,0:T(4,128)S(1)}, f32[4,384]{1,0:T(4,128)S(1)}, u32[]{:S(2)}, u32[]{:S(2)}) %collective-permute-start.32) | collective-permute-done | bytes 6176 | tf_op jit(solution)/shard_map/ppermute | solution.py:444
  211.7 4.7 %combine.7 = bf16[384,2048]{1,0:T(8,128)(2,1)} custom-call(s32[5]{0:T(128)} %pad_add_fusion.facts_ref, bf16[384,2048]{1,0:T(8,128)(2,1)} %combine.6.refs_0_, f32[384,512]{1,0:T(8,128)} %copy-done.5, bf16[384,512]{1,0:T(8,128)(2,1)} %copy-done.18, bf16[384,512]{1,0:T(8,128)(2,1)} %copy-done.20, f32[4,384]{1,0:T(4,128)} %copy-done.11, ...), custom_call_target="tpu_custom_call", output_to_operand_aliasing={{}: (1, {})} | custom-call | flops 3145728 | bytes 1966080 | tf_op jit(solution)/shard_map/combine/pallas_call | solution.py:386
  (95 shorter events, 15.8 us)
Async XLA Ops:
  2.9 10.1 %copy-start.1 = (bf16[384,2048]{1,0:T(8,128)(2,1)S(1)}, bf16[384,2048]{1,0:T(8,128)(2,1)}, u32[]{:S(2)}) copy-start(bf16[384,2048]{1,0:T(8,128)(2,1)} %own_k.7) | copy-start | bytes 4718596
  2.9 22.3 %collective-permute-start = (bf16[128,2048]{1,0:T(8,128)(2,1)}, bf16[128,2048]{1,0:T(8,128)(2,1)}, u32[]{:S(2)}, u32[]{:S(2)}) collective-permute-start(bf16[128,2048]{1,0:T(8,128)(2,1)} %multiply_convert_fusion), channel_id=1, source_target_pairs={{0,4},{4,8},{8,12},{1,5},{5,9},{9,13},{2,6},{6,10},{10,14},{3,7},{... | collective-permute-start | bytes 1572872 | tf_op jit(solution)/shard_map/ppermute | solution.py:17
  5.5 15.8 %copy-start.29 = (s32[4]{0:T(128)S(1)}, s32[4]{0:T(128)}, u32[]{:S(2)}) copy-start(s32[4]{0:T(128)} %param.15) | copy-start | bytes 52
  5.5 16.4 %collective-permute-start.1 = (bf16[384,512]{1,0:T(8,128)(2,1)}, bf16[384,512]{1,0:T(8,128)(2,1)}, u32[]{:S(2)}, u32[]{:S(2)}) collective-permute-start(bf16[384,512]{1,0:T(8,128)(2,1)} %get-tuple-element.61), channel_id=1, source_target_pairs={{8,4},{12,8},{9,5},{13,9},{10,6},{14,10},{11,7},{15,11},{24,20},{2... | collective-permute-start | bytes 1179656 | tf_op jit(solution)/shard_map/ppermute | solution.py:431
  10.9 31.6 %collective-permute-start.2 = (bf16[384,512]{1,0:T(8,128)(2,1)}, bf16[384,512]{1,0:T(8,128)(2,1)}, u32[]{:S(2)}, u32[]{:S(2)}) collective-permute-start(bf16[384,512]{1,0:T(8,128)(2,1)} %get-tuple-element.61), channel_id=1, source_target_pairs={{12,4},{13,5},{14,6},{15,7},{28,20},{29,21},{30,22},{31,23}} | collective-permute-start | bytes 1179656 | tf_op jit(solution)/shard_map/ppermute | solution.py:432
  14.1 29.7 %collective-permute-start.3 = (bf16[384,512]{1,0:T(8,128)(2,1)}, bf16[384,512]{1,0:T(8,128)(2,1)}, u32[]{:S(2)}, u32[]{:S(2)}) collective-permute-start(bf16[384,512]{1,0:T(8,128)(2,1)} %get-tuple-element.57), channel_id=1, source_target_pairs={{0,4},{1,5},{2,6},{3,7},{16,20},{17,21},{18,22},{19,23}} | collective-permute-start | bytes 1179656 | tf_op jit(solution)/shard_map/ppermute | solution.py:430
  15.5 29.6 %collective-permute-start.10 = (bf16[384,512]{1,0:T(8,128)(2,1)}, bf16[384,512]{1,0:T(8,128)(2,1)S(1)}, u32[]{:S(2)}, u32[]{:S(2)}) collective-permute-start(bf16[384,512]{1,0:T(8,128)(2,1)} %get-tuple-element.60), channel_id=1, source_target_pairs={{12,4},{13,5},{14,6},{15,7},{28,20},{29,21},{30,22},{31,23}} | collective-permute-start | bytes 1179656 | tf_op jit(solution)/shard_map/ppermute | solution.py:432
  21.9 25.6 %collective-permute-start.9 = (bf16[384,512]{1,0:T(8,128)(2,1)}, bf16[384,512]{1,0:T(8,128)(2,1)}, u32[]{:S(2)}, u32[]{:S(2)}) collective-permute-start(bf16[384,512]{1,0:T(8,128)(2,1)} %get-tuple-element.60), channel_id=1, source_target_pairs={{8,4},{12,8},{9,5},{13,9},{10,6},{14,10},{11,7},{15,11},{24,20},{2... | collective-permute-start | bytes 1179656 | tf_op jit(solution)/shard_map/ppermute | solution.py:431
  25.2 24.4 %collective-permute-start.11 = (bf16[384,512]{1,0:T(8,128)(2,1)}, bf16[384,512]{1,0:T(8,128)(2,1)}, u32[]{:S(2)}, u32[]{:S(2)}) collective-permute-start(bf16[384,512]{1,0:T(8,128)(2,1)} %get-tuple-element.56), channel_id=1, source_target_pairs={{0,4},{1,5},{2,6},{3,7},{16,20},{17,21},{18,22},{19,23}} | collective-permute-start | bytes 1179656 | tf_op jit(solution)/shard_map/ppermute | solution.py:430
  42.5 11.2 %collective-permute-start.17 = (bf16[384,512]{1,0:T(8,128)(2,1)}, bf16[384,512]{1,0:T(8,128)(2,1)S(1)}, u32[]{:S(2)}, u32[]{:S(2)}) collective-permute-start(bf16[384,512]{1,0:T(8,128)(2,1)} %get-tuple-element.59), channel_id=1, source_target_pairs={{8,4},{12,8},{9,5},{13,9},{10,6},{14,10},{11,7},{15,11},{24,20},{2... | collective-permute-start | bytes 1179656 | tf_op jit(solution)/shard_map/ppermute | solution.py:431
  43.9 18.3 %collective-permute-start.18 = (bf16[384,512]{1,0:T(8,128)(2,1)}, bf16[384,512]{1,0:T(8,128)(2,1)S(1)}, u32[]{:S(2)}, u32[]{:S(2)}) collective-permute-start(bf16[384,512]{1,0:T(8,128)(2,1)} %get-tuple-element.59), channel_id=1, source_target_pairs={{12,4},{13,5},{14,6},{15,7},{28,20},{29,21},{30,22},{31,23}} | collective-permute-start | bytes 1179656 | tf_op jit(solution)/shard_map/ppermute | solution.py:432
  45.2 22.2 %copy-start.13 = (bf16[384,512]{1,0:T(8,128)(2,1)S(1)}, bf16[384,512]{1,0:T(8,128)(2,1)}, u32[]{:S(2)}) copy-start(bf16[384,512]{1,0:T(8,128)(2,1)} %get-tuple-element.54) | copy-start | bytes 1179652
  45.2 26.7 %copy-start.2 = (bf16[384,2048]{1,0:T(8,128)(2,1)S(1)}, bf16[384,2048]{1,0:T(8,128)(2,1)}, u32[]{:S(2)}) copy-start(bf16[384,2048]{1,0:T(8,128)(2,1)} %hyena.1.own_v) | copy-start | bytes 4718596
  45.2 26.7 %copy-start.7 = (s32[5]{0:T(128)S(1)}, s32[5]{0:T(128)}, u32[]{:S(2)}) copy-start(s32[5]{0:T(128)} %pad_add_fusion.facts_ref) | copy-start | bytes 64
  45.2 22.1 %collective-permute-start.19 = (bf16[384,512]{1,0:T(8,128)(2,1)}, bf16[384,512]{1,0:T(8,128)(2,1)S(1)}, u32[]{:S(2)}, u32[]{:S(2)}) collective-permute-start(bf16[384,512]{1,0:T(8,128)(2,1)} %get-tuple-element.55), channel_id=1, source_target_pairs={{0,4},{1,5},{2,6},{3,7},{16,20},{17,21},{18,22},{19,23}} | collective-permute-start | bytes 1179656 | tf_op jit(solution)/shard_map/ppermute | solution.py:430
  47.5 22.9 %collective-permute-start.25 = (bf16[384,512]{1,0:T(8,128)(2,1)S(1)}, bf16[384,512]{1,0:T(8,128)(2,1)S(1)}, u32[]{:S(2)}, u32[]{:S(2)}) collective-permute-start(bf16[384,512]{1,0:T(8,128)(2,1)S(1)} %copy-done.12), channel_id=1, source_target_pairs={{8,4},{12,8},{9,5},{13,9},{10,6},{14,10},{11,7},{15,11},{24,20},{2... | collective-permute-start | bytes 1179656 | tf_op jit(solution)/shard_map/ppermute | solution.py:431
  49.6 21.6 %collective-permute-start.4 = (bf16[384,512]{1,0:T(8,128)(2,1)S(1)}, bf16[384,512]{1,0:T(8,128)(2,1)S(1)}, u32[]{:S(2)}, u32[]{:S(2)}) collective-permute-start(bf16[384,512]{1,0:T(8,128)(2,1)S(1)} %get-tuple-element.53), channel_id=1, source_target_pairs={{0,4},{1,5},{2,6},{3,7},{16,20},{17,21},{18,22},{19,23}} | collective-permute-start | bytes 1179656 | tf_op jit(solution)/shard_map/ppermute | solution.py:433
  53.7 27.6 %collective-permute-start.12 = (bf16[384,512]{1,0:T(8,128)(2,1)S(1)}, bf16[384,512]{1,0:T(8,128)(2,1)S(1)}, u32[]{:S(2)}, u32[]{:S(2)}) collective-permute-start(bf16[384,512]{1,0:T(8,128)(2,1)S(1)} %get-tuple-element.52), channel_id=1, source_target_pairs={{0,4},{1,5},{2,6},{3,7},{16,20},{17,21},{18,22},{19,23}} | collective-permute-start | bytes 1179656 | tf_op jit(solution)/shard_map/ppermute | solution.py:433
  62.2 29.2 %collective-permute-start.26 = (bf16[384,512]{1,0:T(8,128)(2,1)S(1)}, bf16[384,512]{1,0:T(8,128)(2,1)S(1)}, u32[]{:S(2)}, u32[]{:S(2)}) collective-permute-start(bf16[384,512]{1,0:T(8,128)(2,1)S(1)} %copy-done.12), channel_id=1, source_target_pairs={{12,4},{13,5},{14,6},{15,7},{28,20},{29,21},{30,22},{31,23}} | collective-permute-start | bytes 1179656 | tf_op jit(solution)/shard_map/ppermute | solution.py:432
  67.4 25.3 %collective-permute-start.27 = (bf16[384,512]{1,0:T(8,128)(2,1)S(1)}, bf16[384,512]{1,0:T(8,128)(2,1)S(1)}, u32[]{:S(2)}, u32[]{:S(2)}) collective-permute-start(bf16[384,512]{1,0:T(8,128)(2,1)S(1)} %copy-done.13), channel_id=1, source_target_pairs={{0,4},{1,5},{2,6},{3,7},{16,20},{17,21},{18,22},{19,23}} | collective-permute-start | bytes 1179656 | tf_op jit(solution)/shard_map/ppermute | solution.py:430
  70.5 23.5 %collective-permute-start.20 = (bf16[384,512]{1,0:T(8,128)(2,1)S(1)}, bf16[384,512]{1,0:T(8,128)(2,1)S(1)}, u32[]{:S(2)}, u32[]{:S(2)}) collective-permute-start(bf16[384,512]{1,0:T(8,128)(2,1)S(1)} %get-tuple-element.51), channel_id=1, source_target_pairs={{0,4},{1,5},{2,6},{3,7},{16,20},{17,21},{18,22},{19,23}} | collective-permute-start | bytes 1179656 | tf_op jit(solution)/shard_map/ppermute | solution.py:433
  71.2 24.1 %collective-permute-start.28 = (bf16[384,512]{1,0:T(8,128)(2,1)S(1)}, bf16[384,512]{1,0:T(8,128)(2,1)S(1)}, u32[]{:S(2)}, u32[]{:S(2)}) collective-permute-start(bf16[384,512]{1,0:T(8,128)(2,1)S(1)} %get-tuple-element.50), channel_id=1, source_target_pairs={{0,4},{1,5},{2,6},{3,7},{16,20},{17,21},{18,22},{19,23}} | collective-permute-start | bytes 1179656 | tf_op jit(solution)/shard_map/ppermute | solution.py:433
  81.3 86.1 %collective-permute-start.5 = (bf16[384,512]{1,0:T(8,128)(2,1)S(1)}, bf16[384,512]{1,0:T(8,128)(2,1)S(1)}, u32[]{:S(2)}, u32[]{:S(2)}) collective-permute-start(bf16[384,512]{1,0:T(8,128)(2,1)S(1)} %get-tuple-element.27), channel_id=1, source_target_pairs={{4,8},{8,12},{5,9},{9,13},{6,10},{10,14},{7,11},{11,15},{20,24},{2... | collective-permute-start | bytes 1179656 | tf_op jit(solution)/shard_map/ppermute | solution.py:440
  91.4 55.0 %copy-start.3 = (f32[384,512]{1,0:T(8,128)}, f32[384,512]{1,0:T(8,128)S(1)}, u32[]{:S(2)}) copy-start(f32[384,512]{1,0:T(8,128)S(1)} %get-tuple-element.32.refs_1_) | copy-start | bytes 2359300
  91.4 87.1 %collective-permute-start.6 = (bf16[384,512]{1,0:T(8,128)(2,1)S(1)}, bf16[384,512]{1,0:T(8,128)(2,1)S(1)}, u32[]{:S(2)}, u32[]{:S(2)}) collective-permute-start(bf16[384,512]{1,0:T(8,128)(2,1)S(1)} %get-tuple-element.28), channel_id=1, source_target_pairs={{4,12},{5,13},{6,14},{7,15},{20,28},{21,29},{22,30},{23,31}} | collective-permute-start | bytes 1179656 | tf_op jit(solution)/shard_map/ppermute | solution.py:441
  92.7 87.1 %collective-permute-start.13 = (bf16[384,512]{1,0:T(8,128)(2,1)S(1)}, bf16[384,512]{1,0:T(8,128)(2,1)S(1)}, u32[]{:S(2)}, u32[]{:S(2)}) collective-permute-start(bf16[384,512]{1,0:T(8,128)(2,1)S(1)} %get-tuple-element.33), channel_id=1, source_target_pairs={{4,8},{8,12},{5,9},{9,13},{6,10},{10,14},{7,11},{11,15},{20,24},{2... | collective-permute-start | bytes 1179656 | tf_op jit(solution)/shard_map/ppermute | solution.py:440
  94.0 18.7 %collective-permute-start.7 = (f32[4,384]{1,0:T(4,128)S(1)}, f32[4,384]{1,0:T(4,128)S(1)}, u32[]{:S(2)}, u32[]{:S(2)}) collective-permute-start(f32[4,384]{1,0:T(4,128)S(1)} %get-tuple-element.30), channel_id=1, source_target_pairs={{4,8},{8,12},{5,9},{9,13},{6,10},{10,14},{7,11},{11,15},{20,24},{2... | collective-permute-start | bytes 18440 | tf_op jit(solution)/shard_map/ppermute | solution.py:443
  95.3 41.8 %collective-permute-start.8 = (f32[4,384]{1,0:T(4,128)S(1)}, f32[4,384]{1,0:T(4,128)S(1)}, u32[]{:S(2)}, u32[]{:S(2)}) collective-permute-start(f32[4,384]{1,0:T(4,128)S(1)} %get-tuple-element.31), channel_id=1, source_target_pairs={{4,12},{5,13},{6,14},{7,15},{20,28},{21,29},{22,30},{23,31}} | collective-permute-start | bytes 18440 | tf_op jit(solution)/shard_map/ppermute | solution.py:444
  112.7 33.7 %copy-start.21 = (f32[4,384]{1,0:T(4,128)}, f32[4,384]{1,0:T(4,128)S(1)}, u32[]{:S(2)}) copy-start(f32[4,384]{1,0:T(4,128)S(1)} %collective-permute-done.7.refs_4_) | copy-start | bytes 18436
  112.7 34.3 %collective-permute-start.15 = (f32[4,384]{1,0:T(4,128)S(1)}, f32[4,384]{1,0:T(4,128)S(1)}, u32[]{:S(2)}, u32[]{:S(2)}) collective-permute-start(f32[4,384]{1,0:T(4,128)S(1)} %get-tuple-element.36), channel_id=1, source_target_pairs={{4,8},{8,12},{5,9},{9,13},{6,10},{10,14},{7,11},{11,15},{20,24},{2... | collective-permute-start | bytes 18440 | tf_op jit(solution)/shard_map/ppermute | solution.py:443
  137.7 10.6 %collective-permute-start.16 = (f32[4,384]{1,0:T(4,128)S(1)}, f32[4,384]{1,0:T(4,128)S(1)}, u32[]{:S(2)}, u32[]{:S(2)}) collective-permute-start(f32[4,384]{1,0:T(4,128)S(1)} %get-tuple-element.37), channel_id=1, source_target_pairs={{4,12},{5,13},{6,14},{7,15},{20,28},{21,29},{22,30},{23,31}} | collective-permute-start | bytes 18440 | tf_op jit(solution)/shard_map/ppermute | solution.py:444
  147.0 30.0 %copy-start.4 = (f32[384,512]{1,0:T(8,128)}, f32[384,512]{1,0:T(8,128)S(1)}, u32[]{:S(2)}) copy-start(f32[384,512]{1,0:T(8,128)S(1)} %get-tuple-element.38.refs_1_) | copy-start | bytes 2359300
  147.0 20.5 %copy-start.23 = (f32[4,384]{1,0:T(4,128)}, f32[4,384]{1,0:T(4,128)S(1)}, u32[]{:S(2)}) copy-start(f32[4,384]{1,0:T(4,128)S(1)} %collective-permute-done.15.refs_5_) | copy-start | bytes 18436
  147.0 9.3 %collective-permute-start.23 = (f32[4,384]{1,0:T(4,128)S(1)}, f32[4,384]{1,0:T(4,128)S(1)}, u32[]{:S(2)}, u32[]{:S(2)}) collective-permute-start(f32[4,384]{1,0:T(4,128)S(1)} %get-tuple-element.42), channel_id=1, source_target_pairs={{4,8},{8,12},{5,9},{9,13},{6,10},{10,14},{7,11},{11,15},{20,24},{2... | collective-permute-start | bytes 18440 | tf_op jit(solution)/shard_map/ppermute | solution.py:443
  148.3 19.2 %copy-start.24 = (f32[4,384]{1,0:T(4,128)}, f32[4,384]{1,0:T(4,128)S(1)}, u32[]{:S(2)}) copy-start(f32[4,384]{1,0:T(4,128)S(1)} %collective-permute-done.16.refs_6_) | copy-start | bytes 18436
  148.3 17.9 %collective-permute-start.24 = (f32[4,384]{1,0:T(4,128)S(1)}, f32[4,384]{1,0:T(4,128)S(1)}, u32[]{:S(2)}, u32[]{:S(2)}) collective-permute-start(f32[4,384]{1,0:T(4,128)S(1)} %get-tuple-element.43), channel_id=1, source_target_pairs={{4,12},{5,13},{6,14},{7,15},{20,28},{21,29},{22,30},{23,31}} | collective-permute-start | bytes 18440 | tf_op jit(solution)/shard_map/ppermute | solution.py:444
  156.2 20.7 %copy-start.25 = (f32[4,384]{1,0:T(4,128)}, f32[4,384]{1,0:T(4,128)S(1)}, u32[]{:S(2)}) copy-start(f32[4,384]{1,0:T(4,128)S(1)} %collective-permute-done.23.refs_5_) | copy-start | bytes 18436
  156.2 24.9 %collective-permute-start.14 = (bf16[384,512]{1,0:T(8,128)(2,1)S(1)}, bf16[384,512]{1,0:T(8,128)(2,1)S(1)}, u32[]{:S(2)}, u32[]{:S(2)}) collective-permute-start(bf16[384,512]{1,0:T(8,128)(2,1)S(1)} %get-tuple-element.34), channel_id=1, source_target_pairs={{4,12},{5,13},{6,14},{7,15},{20,28},{21,29},{22,30},{23,31}} | collective-permute-start | bytes 1179656 | tf_op jit(solution)/shard_map/ppermute | solution.py:441
  166.2 18.1 %collective-permute-start.21 = (bf16[384,512]{1,0:T(8,128)(2,1)S(1)}, bf16[384,512]{1,0:T(8,128)(2,1)S(1)}, u32[]{:S(2)}, u32[]{:S(2)}) collective-permute-start(bf16[384,512]{1,0:T(8,128)(2,1)S(1)} %get-tuple-element.39), channel_id=1, source_target_pairs={{4,8},{8,12},{5,9},{9,13},{6,10},{10,14},{7,11},{11,15},{20,24},{2... | collective-permute-start | bytes 1179656 | tf_op jit(solution)/shard_map/ppermute | solution.py:440
  167.5 9.5 %copy-start.14 = (bf16[384,512]{1,0:T(8,128)(2,1)}, bf16[384,512]{1,0:T(8,128)(2,1)S(1)}, u32[]{:S(2)}) copy-start(bf16[384,512]{1,0:T(8,128)(2,1)S(1)} %collective-permute-done.5.refs_1_) | copy-start | bytes 1179652
  167.5 27.5 %collective-permute-start.22 = (bf16[384,512]{1,0:T(8,128)(2,1)S(1)}, bf16[384,512]{1,0:T(8,128)(2,1)}, u32[]{:S(2)}, u32[]{:S(2)}) collective-permute-start(bf16[384,512]{1,0:T(8,128)(2,1)S(1)} %get-tuple-element.40), channel_id=1, source_target_pairs={{4,12},{5,13},{6,14},{7,15},{20,28},{21,29},{22,30},{23,31}} | collective-permute-start | bytes 1179656 | tf_op jit(solution)/shard_map/ppermute | solution.py:441
  178.5 7.0 %copy-start.15 = (bf16[384,512]{1,0:T(8,128)(2,1)}, bf16[384,512]{1,0:T(8,128)(2,1)S(1)}, u32[]{:S(2)}) copy-start(bf16[384,512]{1,0:T(8,128)(2,1)S(1)} %collective-permute-done.6.refs_2_) | copy-start | bytes 1179652
  178.5 32.4 %collective-permute-start.29 = (bf16[384,512]{1,0:T(8,128)(2,1)}, bf16[384,512]{1,0:T(8,128)(2,1)S(1)}, u32[]{:S(2)}, u32[]{:S(2)}) collective-permute-start(bf16[384,512]{1,0:T(8,128)(2,1)} %get-tuple-element.45), channel_id=1, source_target_pairs={{4,8},{8,12},{5,9},{9,13},{6,10},{10,14},{7,11},{11,15},{20,24},{2... | collective-permute-start | bytes 1179656 | tf_op jit(solution)/shard_map/ppermute | solution.py:440
  179.8 5.7 %copy-start.16 = (bf16[384,512]{1,0:T(8,128)(2,1)}, bf16[384,512]{1,0:T(8,128)(2,1)S(1)}, u32[]{:S(2)}) copy-start(bf16[384,512]{1,0:T(8,128)(2,1)S(1)} %collective-permute-done.13.refs_2_) | copy-start | bytes 1179652
  179.8 31.1 %collective-permute-start.30 = (bf16[384,512]{1,0:T(8,128)(2,1)}, bf16[384,512]{1,0:T(8,128)(2,1)S(1)}, u32[]{:S(2)}, u32[]{:S(2)}) collective-permute-start(bf16[384,512]{1,0:T(8,128)(2,1)} %get-tuple-element.46), channel_id=1, source_target_pairs={{4,12},{5,13},{6,14},{7,15},{20,28},{21,29},{22,30},{23,31}} | collective-permute-start | bytes 1179656 | tf_op jit(solution)/shard_map/ppermute | solution.py:441
  181.1 18.9 %collective-permute-start.31 = (f32[4,384]{1,0:T(4,128)}, f32[4,384]{1,0:T(4,128)S(1)}, u32[]{:S(2)}, u32[]{:S(2)}) collective-permute-start(f32[4,384]{1,0:T(4,128)} %get-tuple-element.48), channel_id=1, source_target_pairs={{4,8},{8,12},{5,9},{9,13},{6,10},{10,14},{7,11},{11,15},{20,24},{2... | collective-permute-start | bytes 18440 | tf_op jit(solution)/shard_map/ppermute | solution.py:443
  184.2 26.6 %collective-permute-start.32 = (f32[4,384]{1,0:T(4,128)S(1)}, f32[4,384]{1,0:T(4,128)S(1)}, u32[]{:S(2)}, u32[]{:S(2)}) collective-permute-start(f32[4,384]{1,0:T(4,128)S(1)} %get-tuple-element.49), channel_id=1, source_target_pairs={{4,12},{5,13},{6,14},{7,15},{20,28},{21,29},{22,30},{23,31}} | collective-permute-start | bytes 18440 | tf_op jit(solution)/shard_map/ppermute | solution.py:444
  200.0 10.9 %copy-start.27 = (f32[4,384]{1,0:T(4,128)}, f32[4,384]{1,0:T(4,128)S(1)}, u32[]{:S(2)}) copy-start(f32[4,384]{1,0:T(4,128)S(1)} %collective-permute-done.31.refs_5_) | copy-start | bytes 18436
  (15 other events, 20.1 us)

commit v2 on v1

--- a/solution.py
+++ b/solution.py
@@ -227,102 +227,100 @@
     )(facts, query, key, value, halo, turned_taps, skip_gain)
 
 
-def attend_tile(queries, keys, values, query_first, key_first, facts_ref, genomes, carried):
-    scores = lax.dot_general(
+def attend_block(queries, keys, values, bias):
+    scores = bias + lax.dot_general(
         queries, keys, (((1,), (1,)), ((), ())), preferred_element_type=jnp.float32
     )
-    query_pos = query_first + lax.broadcasted_iota(jnp.int32, (queries.shape[0], 1), 0)
-    begin = begin_of(query_pos, facts_ref, genomes)
-    key_pos = key_first + lax.broadcasted_iota(jnp.int32, scores.shape, 1)
-    visible = (key_pos >= begin) & (key_pos <= query_pos)
-    scores = jnp.where(visible, scores, 10 * NEVER)
-    highest, total, mixed = carried
-    new_highest = jnp.maximum(highest, jnp.max(scores, axis=1, keepdims=True))
-    weights = jnp.exp2((scores - new_highest) * EXPONENT)
-    fade = jnp.exp2((highest - new_highest) * EXPONENT)
-    new_mixed = fade * mixed + jnp.dot(
-        weights.astype(jnp.bfloat16), values, preferred_element_type=jnp.float32
-    )
-    return new_highest, fade * total + jnp.sum(weights, axis=1, keepdims=True), new_mixed
+    highest = jnp.maximum(jnp.max(scores, axis=1, keepdims=True), NEVER)
+    weights = jnp.exp2((scores - highest) * EXPONENT).astype(jnp.bfloat16)
+    mixed = jnp.dot(weights, values, preferred_element_type=jnp.float32)
+    summed = mixed[:, HEAD_DIM:]
+    some = summed > 0
+    safe = jnp.where(some, summed, 1.0)
+    log = jnp.where(some, highest * EXPONENT + jnp.log2(safe), NEVER)
+    return mixed[:, :HEAD_DIM] / safe, log
 
 
 def attend_kernel(genomes, facts_ref, own_q, next_q, last_q, own_k, own_v, far_k, far_v,
-                  own_o, next_o, last_o, own_l, next_l, last_l, high, total, mixed):
+                  own_o, next_o, last_o, own_l, next_l, last_l, queries, keys, values, bias,
+                  mixed, logs):
     rows = own_q.shape[0]
+    per_shard = rows // BLOCK
     head = pl.program_id(0)
     shard = facts_ref[genomes]
     own_first = shard * rows
-
-    def update(here, queries, keys, values, query_first, key_first):
-        carried = (high[here], total[here], mixed[here])
-        high[here], total[here], mixed[here] = attend_tile(
-            queries, keys, values, query_first, key_first, facts_ref, genomes, carried
-        )
-
-    def clear():
-        high[...] = jnp.full_like(high, NEVER)
-        total[...] = jnp.zeros_like(total)
-        mixed[...] = jnp.zeros_like(mixed)
-
-    def finish(out_ref, log_ref):
-        summed = total[...]
-        some = summed > 0
-        safe = jnp.where(some, summed, 1.0)
-        out_ref[...] = (mixed[...] / safe).astype(out_ref.dtype)
-        log = jnp.where(some, high[...] * EXPONENT + jnp.log2(safe), NEVER)
-        log_ref[pl.ds(head, 1), :] = jnp.transpose(jnp.broadcast_to(log, (rows, BLOCK)))[:1]
-
-    everything = slice(0, rows)
-
-    def reach(query_first):
-        begin = jnp.int32(0)
+    base = own_first - rows
+    limit = jnp.where(shard == 1, base, own_first)
+    steps = per_shard * jnp.where(shard == 1, 3, jnp.where(shard == 2, 2, 1))
+
+    def rows_of(step):
+        return pl.ds(pl.multiple_of(step * BLOCK, BLOCK), BLOCK)
+
+    @pl.when(head == 0)
+    def _():
+        values[:, HEAD_DIM:] = jnp.ones((2 * rows, HEAD_DIM), jnp.bfloat16)
+        logs[...] = jnp.full_like(logs, NEVER)
+
+        def fill(step, nothing):
+            query_pos = own_first + step * BLOCK + lax.broadcasted_iota(jnp.int32, (BLOCK, 1), 0)
+            begin = jnp.maximum(begin_of(query_pos, facts_ref, genomes), limit)
+            key_pos = base + lax.broadcasted_iota(jnp.int32, (BLOCK, 2 * rows), 1)
+            visible = (key_pos >= begin) & (key_pos <= query_pos)
+            bias[rows_of(step), :] = jnp.where(visible, 0.0, 10 * NEVER)
+            return nothing
+
+        lax.fori_loop(0, steps, fill, 0)
+
+    for slot, ref in enumerate((own_q, next_q, last_q)):
+        queries[slot * rows : (slot + 1) * rows] = ref[...]
+    for slot, (k_ref, v_ref) in enumerate(((far_k, far_v), (own_k, own_v))):
+        here = slice(slot * rows, (slot + 1) * rows)
+        keys[here] = k_ref[...]
+        values[here, :HEAD_DIM] = v_ref[...]
+
+    def one_step(step, nothing):
+        query_first = own_first + step * BLOCK
+        begin = limit
         for genome in range(genomes):
             start = facts_ref[genome]
             begin = jnp.where(start <= query_first, jnp.maximum(begin, start), begin)
-        return begin
-
-    clear()
-
-    @pl.when((shard == 1) & (reach(own_first) < rows))
+        first = (begin - base) // BLOCK
+        last = jnp.minimum(query_first + BLOCK, own_first + rows)
+        count = (last - base) // BLOCK - first
+
+        @pl.when(count <= 0)
+        def _():
+            mixed[rows_of(step), :] = jnp.zeros((BLOCK, HEAD_DIM), jnp.float32)
+
+        for blocks in range(1, 2 * per_shard + 1):
+
+            @pl.when(count == blocks)
+            def _():
+                span = pl.ds(pl.multiple_of(first * BLOCK, BLOCK), blocks * BLOCK)
+                out, log = attend_block(
+                    queries[rows_of(step), :], keys[span, :], values[span, :], bias[rows_of(step), span]
+                )
+                mixed[rows_of(step), :] = out
+                lane = lax.broadcasted_iota(jnp.int32, (BLOCK, BLOCK), 1)
+                logs[rows_of(step), :] = jnp.where(lane == head, log, logs[rows_of(step), :])
+
+        return nothing
+
+    lax.fori_loop(0, steps, one_step, 0)
+    for slot, ref in enumerate((own_o, next_o, last_o)):
+        ref[...] = mixed[slot * rows : (slot + 1) * rows].astype(ref.dtype)
+
+    @pl.when(head == pl.num_programs(0) - 1)
     def _():
-        update(everything, own_q[...], far_k[...], far_v[...], own_first, 0)
-
-    for b in range(rows // BLOCK):
-        here = slice(b * BLOCK, (b + 1) * BLOCK)
-        upto = slice(0, (b + 1) * BLOCK)
-        update(here, own_q[here], own_k[upto], own_v[upto], own_first + b * BLOCK, own_first)
-    finish(own_o, own_l)
-
-    for queries, query_shard, used, out_ref, log_ref in (
-        (next_q, shard + 1, (shard == 1) | (shard == 2), next_o, next_l),
-        (last_q, 3, shard == 1, last_o, last_l),
-    ):
-        query_first = query_shard * rows
-        begin = reach(query_first)
-        needed = used & (begin < own_first + rows)
-
-        @pl.when(needed)
-        def _():
-            clear()
-            update(everything, queries[...], own_k[...], own_v[...], query_first, own_first)
-
-            @pl.when((shard == 1) & (begin < rows))
-            def _():
-                update(everything, queries[...], far_k[...], far_v[...], query_first, 0)
-
-            finish(out_ref, log_ref)
-
-        @pl.when(jnp.logical_not(needed))
-        def _():
-            out_ref[...] = jnp.zeros_like(out_ref)
-            log_ref[pl.ds(head, 1), :] = jnp.full((1, rows), NEVER, jnp.float32)
+        for slot, ref in enumerate((own_l, next_l, last_l)):
+            ref[...] = jnp.transpose(logs[slot * rows : (slot + 1) * rows])[:8]
 
 
 def attend(facts, genomes, chunk, heads, own_q, next_q, last_q, own_k, own_v, far_k, far_v):
     rows = own_q.shape[0]
     whole = pl.BlockSpec((rows, HEAD_DIM), lambda h, facts_ref: (0, chunk * heads + h))
     piece = pl.BlockSpec((rows, HEAD_DIM), lambda h, facts_ref: (0, h))
-    logs = pl.BlockSpec((heads, rows), lambda h, facts_ref: (0, 0))
+    logs = pl.BlockSpec((8, rows), lambda h, facts_ref: (0, 0))
     width = heads * HEAD_DIM
     return pl.pallas_call(
         partial(attend_kernel, genomes),
@@ -330,9 +328,9 @@
             jax.ShapeDtypeStruct((rows, width), jnp.float32),
             jax.ShapeDtypeStruct((rows, width), jnp.bfloat16),
             jax.ShapeDtypeStruct((rows, width), jnp.bfloat16),
-            jax.ShapeDtypeStruct((heads, rows), jnp.float32),
-            jax.ShapeDtypeStruct((heads, rows), jnp.float32),
-            jax.ShapeDtypeStruct((heads, rows), jnp.float32),
+            jax.ShapeDtypeStruct((8, rows), jnp.float32),
+            jax.ShapeDtypeStruct((8, rows), jnp.float32),
+            jax.ShapeDtypeStruct((8, rows), jnp.float32),
         ),
         grid_spec=pltpu.PrefetchScalarGridSpec(
             num_scalar_prefetch=1,
@@ -340,16 +338,19 @@
             in_specs=[whole, piece, piece, whole, whole, piece, piece],
             out_specs=[piece, piece, piece, logs, logs, logs],
             scratch_shapes=[
-                pltpu.VMEM((rows, 1), jnp.float32),
-                pltpu.VMEM((rows, 1), jnp.float32),
-                pltpu.VMEM((rows, HEAD_DIM), jnp.float32),
+                pltpu.VMEM((3 * rows, HEAD_DIM), jnp.bfloat16),
+                pltpu.VMEM((2 * rows, HEAD_DIM), jnp.bfloat16),
+                pltpu.VMEM((2 * rows, 2 * HEAD_DIM), jnp.bfloat16),
+                pltpu.VMEM((3 * rows, 2 * rows), jnp.float32),
+                pltpu.VMEM((3 * rows, HEAD_DIM), jnp.float32),
+                pltpu.VMEM((3 * rows, BLOCK), jnp.float32),
             ],
         ),
         compiler_params=pltpu.CompilerParams(vmem_limit_bytes=32 << 20),
         cost_estimate=pl.CostEstimate(
-            flops=24 * rows * rows * width,
+            flops=12 * rows * rows * width,
             bytes_accessed=rows * width * 22,
-            transcendentals=6 * rows * rows * heads,
+            transcendentals=3 * rows * rows * heads,
         ),
         name="attend",
     )(facts, own_q, next_q, last_q, own_k, own_v, far_k, far_v)
@@ -358,41 +359,40 @@
 def combine_kernel(genomes, facts_ref, *refs):
     own_o, near_o, far_o, own_l, near_l, far_l = refs[-7:-1]
     out_ref = refs[-1]
-    rows = own_o.shape[0]
-    head = pl.program_id(0)
+    width = own_o.shape[1]
     shard = facts_ref[genomes]
-
-    def column(log_ref):
-        return jnp.transpose(jnp.broadcast_to(log_ref[pl.ds(head, 1), :], (BLOCK, rows)))
-
-    own = column(own_l)
-    near = jnp.where(shard >= 2, column(near_l), NEVER)
-    far = jnp.where(shard == 3, column(far_l), NEVER)
+    own = own_l[...]
+    near = jnp.where(shard >= 2, near_l[...], NEVER)
+    far = jnp.where(shard == 3, far_l[...], NEVER)
     highest = jnp.maximum(own, jnp.maximum(near, far))
-    own, near, far = jnp.exp2(own - highest), jnp.exp2(near - highest), jnp.exp2(far - highest)
-    mixed = (
-        own * own_o[...]
-        + near * near_o[...].astype(jnp.float32)
-        + far * far_o[...].astype(jnp.float32)
-    )
-    out_ref[...] = (mixed / (own + near + far)).astype(out_ref.dtype)
+    shares = [jnp.exp2(log - highest) for log in (own, near, far)]
+    whole = shares[0] + shares[1] + shares[2]
+    columns = [
+        jnp.transpose(jnp.concatenate([share / whole] + [jnp.zeros((BLOCK - 8, BLOCK), jnp.float32)]))
+        for share in shares
+    ]
+    for head in range(width // HEAD_DIM):
+        here = slice(head * HEAD_DIM, (head + 1) * HEAD_DIM)
+        mixed = columns[0][:, head : head + 1] * own_o[:, here]
+        for column, ref in ((columns[1], near_o), (columns[2], far_o)):
+            mixed += column[:, head : head + 1] * ref[:, here].astype(jnp.float32)
+        out_ref[:, here] = mixed.astype(out_ref.dtype)
 
 
 def combine(facts, genomes, chunk, heads, channels, earlier, *pieces):
     rows = pieces[0].shape[0]
-    piece = pl.BlockSpec((rows, HEAD_DIM), lambda h, facts_ref: (0, h))
-    logs = pl.BlockSpec((heads, rows), lambda h, facts_ref: (0, 0))
+    width = heads * HEAD_DIM
+    piece = pl.BlockSpec((BLOCK, width), lambda r, facts_ref: (r, 0))
+    logs = pl.BlockSpec((8, BLOCK), lambda r, facts_ref: (0, r))
     held = () if earlier is None else (earlier,)
     return pl.pallas_call(
         partial(combine_kernel, genomes),
         out_shape=jax.ShapeDtypeStruct((rows, channels), jnp.bfloat16),
         grid_spec=pltpu.PrefetchScalarGridSpec(
             num_scalar_prefetch=1,
-            grid=(heads,),
+            grid=(rows // BLOCK,),
             in_specs=[pl.BlockSpec(memory_space=pl.ANY)] * len(held) + [piece] * 3 + [logs] * 3,
-            out_specs=pl.BlockSpec(
-                (rows, HEAD_DIM), lambda h, facts_ref: (0, chunk * heads + h)
-            ),
+            out_specs=pl.BlockSpec((BLOCK, width), lambda r, facts_ref: (r, chunk)),
         ),
         input_output_aliases={1: 0} if held else {},
         cost_estimate=pl.CostEstimate(

time: 220 us -> 212 us (0.964); the launches traced: 216 us -> 213 us
  waiting for transfers between devices: 81.1 us -> 72.5 us
  starting transfers between devices: 51.3 us -> 54.6 us
    ppermute x4, starting transfers between devices: 9.87 us -> 14.5 us  [balanced_plan(): last_q = lax.ppermute(queries, 'ctx', [(3, 1)])]
    ppermute x4, waiting for transfers between devices: 5.85 us -> 2.41 us  [balanced_plan(): next_q = lax.ppermute(queries, 'ctx', [(2, 1), (3, 2)])]
    ppermute x4, waiting for transfers between devices: 42.6 us -> 39.4 us  [balanced_plan(): lax.ppermute(last_l, 'ctx', [(1, 3)])]
    pallas_call x4, Pallas kernels: 31.2 us -> 34.2 us  [attend(): pl.pallas_call(partial(attend_kernel, genomes), out_shape=(jax.ShapeDtype...]
    unnamed x60 -> x64, local copies, waits for them, and re-layouts: 5.67 us -> 5.56 us
  transfers between devices with their start and end apart: 33 -> 33, of which waited for: 10 -> 10; matrix products, arithmetic and copies ran while one was open for 4% -> 4% of each run, Pallas kernels for 28% -> 30%
where the time goes in v2:
time: 212 us; the launch traced here: 213 us
  waiting for transfers between devices  72.5 us (34%)
  Pallas kernels  67.8 us (32%)
  starting transfers between devices  54.6 us (26%)
  local copies, waits for them, and re-layouts  12.3 us (6%)
  other arithmetic  4.31 us (2%)
    ppermute x4, waiting for transfers between devices, balanced_plan(): lax.ppermute(last_l, 'ctx', [(1, 3)])  39.4 us
    pallas_call x4, Pallas kernels, attend(): pl.pallas_call(partial(attend_kernel, genomes), out_shape=(jax.ShapeDtype...  34.2 us
    ppermute x4, waiting for transfers between devices, balanced_plan(): lax.ppermute(next_l, 'ctx', [(1, 2), (2, 3)])  22.4 us
    pallas_call x4, Pallas kernels, combine(): pl.pallas_call(partial(combine_kernel, genomes), out_shape=jax.ShapeDtype...  17.6 us
    pallas_call x1, Pallas kernels, hyena(): pl.pallas_call(partial(hyena_kernel, genomes), out_shape=jax.ShapeDtypeSt...  16 us
    ppermute x4, starting transfers between devices, balanced_plan(): last_q = lax.ppermute(queries, 'ctx', [(3, 1)])  14.5 us
    ppermute x4, starting transfers between devices, balanced_plan(): next_q = lax.ppermute(queries, 'ctx', [(2, 1), (3, 2)])  11.1 us
    ppermute x4, waiting for transfers between devices, balanced_plan(): last_q = lax.ppermute(queries, 'ctx', [(3, 1)])  6.9 us
  transfers between devices with their start and end apart: 33, of which 10 were waited for; matrix products, arithmetic and copies ran while one was open for 4% of the time, Pallas kernels for 30%

profile of v2, /device:TPU:30, one launch (start us, length us, event | category | flops | bytes accessed | tf_op | source)
XLA Modules:
  0.0 212.8 jit_solution(10891726904725624241)
XLA Ops:
  0.6 2.2 %multiply_convert_fusion = bf16[128,2048]{1,0:T(8,128)(2,1)} fusion(bf16[384,2048]{1,0:T(8,128)(2,1)} %value_ref.1, bf16[384,2048]{1,0:T(8,128)(2,1)} %key_ref.1), kind=kLoop, calls=%fused_computation | loop fusion | flops 1048576 | bytes 1572864 | tf_op jit(solution)/shard_map/convert_element_type | solution.py:417
  2.9 1.4 collective-permute-start
  5.5 4.7 %collective-permute-start.1 = (bf16[384,512]{1,0:T(8,128)(2,1)}, bf16[384,512]{1,0:T(8,128)(2,1)S(1)}, u32[]{:S(2)}, u32[]{:S(2)}) collective-permute-start(bf16[384,512]{1,0:T(8,128)(2,1)} %get-tuple-element.61), channel_id=1, source_target_pairs={{8,4},{12,8},{9,5},{13,9},{10,6},{14,10},{11,7},{15,11},{24,20},{2... | collective-permute-start | bytes 1179656 | tf_op jit(solution)/shard_map/ppermute | solution.py:431
  10.2 2.1 collective-permute-start.2
  13.5 1.4 collective-permute-start.3
  14.9 2.0 collective-permute-start.10
  16.9 1.4 slice.57
  18.3 1.4 slice.58
  19.8 1.5 maximum_convert_fusion.taps_ref
  22.6 3.2 %collective-permute-start.9 = (bf16[384,512]{1,0:T(8,128)(2,1)}, bf16[384,512]{1,0:T(8,128)(2,1)}, u32[]{:S(2)}, u32[]{:S(2)}) collective-permute-start(bf16[384,512]{1,0:T(8,128)(2,1)} %get-tuple-element.60), channel_id=1, source_target_pairs={{8,4},{12,8},{9,5},{13,9},{10,6},{14,10},{11,7},{15,11},{24,20},{2... | collective-permute-start | bytes 1179656 | tf_op jit(solution)/shard_map/ppermute | solution.py:431
  25.8 2.7 %collective-permute-done.2.last_q = bf16[384,512]{1,0:T(8,128)(2,1)} collective-permute-done((bf16[384,512]{1,0:T(8,128)(2,1)}, bf16[384,512]{1,0:T(8,128)(2,1)}, u32[]{:S(2)}, u32[]{:S(2)}) %collective-permute-start.2) | collective-permute-done | bytes 393248 | tf_op jit(solution)/shard_map/ppermute | solution.py:432
  28.5 1.4 collective-permute-start.11
  29.9 1.3 collective-permute-start.17
  31.2 16.0 %hyena.1.own_v = bf16[384,2048]{1,0:T(8,128)(2,1)} custom-call(s32[5]{0:T(128)} %pad_add_fusion.facts_ref, bf16[384,2048]{1,0:T(8,128)(2,1)} %query_ref.1, bf16[384,2048]{1,0:T(8,128)(2,1)} %key_ref.1, bf16[384,2048]{1,0:T(8,128)(2,1)} %value_ref.1, bf16[128,2048]{1,0:T(8,128)(2,1)} %collective-permute-done.halo_ref, ...), custom_call_target="tpu_custom_call" | custom-call | flops 3221225472 | bytes 6291456 | tf_op jit(solution)/shard_map/hyena/pallas_call | solution.py:201
  47.2 5.2 %collective-permute-start.18 = (bf16[384,512]{1,0:T(8,128)(2,1)}, bf16[384,512]{1,0:T(8,128)(2,1)S(1)}, u32[]{:S(2)}, u32[]{:S(2)}) collective-permute-start(bf16[384,512]{1,0:T(8,128)(2,1)} %get-tuple-element.59), channel_id=1, source_target_pairs={{12,4},{13,5},{14,6},{15,7},{28,20},{29,21},{30,22},{31,23}} | collective-permute-start | bytes 1179656 | tf_op jit(solution)/shard_map/ppermute | solution.py:432
  53.3 1.5 fusion
  54.8 1.9 collective-permute-start.25
  58.1 4.2 %collective-permute-done.18.last_q = bf16[384,512]{1,0:T(8,128)(2,1)S(1)} collective-permute-done((bf16[384,512]{1,0:T(8,128)(2,1)}, bf16[384,512]{1,0:T(8,128)(2,1)S(1)}, u32[]{:S(2)}, u32[]{:S(2)}) %collective-permute-start.18) | collective-permute-done | bytes 393248 | tf_op jit(solution)/shard_map/ppermute | solution.py:432
  62.3 5.2 %collective-permute-start.26 = (bf16[384,512]{1,0:T(8,128)(2,1)S(1)}, bf16[384,512]{1,0:T(8,128)(2,1)S(1)}, u32[]{:S(2)}, u32[]{:S(2)}) collective-permute-start(bf16[384,512]{1,0:T(8,128)(2,1)S(1)} %copy-done.14), channel_id=1, source_target_pairs={{12,4},{13,5},{14,6},{15,7},{28,20},{29,21},{30,22},{31,23}} | collective-permute-start | bytes 1179656 | tf_op jit(solution)/shard_map/ppermute | solution.py:432
  68.2 2.4 %collective-permute-done.25.next_q = bf16[384,512]{1,0:T(8,128)(2,1)S(1)} collective-permute-done((bf16[384,512]{1,0:T(8,128)(2,1)S(1)}, bf16[384,512]{1,0:T(8,128)(2,1)S(1)}, u32[]{:S(2)}, u32[]{:S(2)}) %collective-permute-start.25) | collective-permute-done | bytes 393248 | tf_op jit(solution)/shard_map/ppermute | solution.py:431
  72.0 8.5 %attend.4 = (f32[384,512]{1,0:T(8,128)S(1)}, bf16[384,512]{1,0:T(8,128)(2,1)S(1)}, bf16[384,512]{1,0:T(8,128)(2,1)S(1)}, f32[8,384]{1,0:T(8,128)S(1)}, f32[8,384]{1,0:T(8,128)S(1)}, /*index=5*/f32[8,384]{1,0:T(8,128)S(1)}) custom-call(s32[5]{0:T(128)S(1)} %copy-done.9, bf16[384,2048]{1,0:T(8,128)(2,1)S(1)} %copy-done, bf16[384,512]{1,0:T(8,128)(2,1)S(1)} %copy-done.8, ...), custom_call_target="tpu_custom_call" | custom-call | flops 905969664 | bytes 4325376 | tf_op jit(solution)/shard_map/attend/pallas_call | solution.py:325
  81.2 1.3 collective-permute-start.5
  82.5 8.5 %attend.5 = (f32[384,512]{1,0:T(8,128)S(1)}, bf16[384,512]{1,0:T(8,128)(2,1)S(1)}, bf16[384,512]{1,0:T(8,128)(2,1)S(1)}, f32[8,384]{1,0:T(8,128)S(1)}, f32[8,384]{1,0:T(8,128)S(1)}, /*index=5*/f32[8,384]{1,0:T(8,128)S(1)}) custom-call(s32[5]{0:T(128)S(1)} %copy-done.9, bf16[384,2048]{1,0:T(8,128)(2,1)S(1)} %copy-done, ...), custom_call_target="tpu_custom_call" | custom-call | flops 905969664 | bytes 4325376 | tf_op jit(solution)/shard_map/attend/pallas_call | solution.py:325
  91.6 1.3 collective-permute-start.6
  92.9 1.3 collective-permute-start.13
  94.2 1.3 collective-permute-start.7
  95.5 1.3 collective-permute-start.8
  96.8 14.3 %collective-permute-done.7.refs_4_ = f32[8,384]{1,0:T(8,128)S(1)} collective-permute-done((f32[8,384]{1,0:T(8,128)S(1)}, f32[8,384]{1,0:T(8,128)S(1)}, u32[]{:S(2)}, u32[]{:S(2)}) %collective-permute-start.7) | collective-permute-done | bytes 12320 | tf_op jit(solution)/shard_map/ppermute | solution.py:443
  111.2 1.3 collective-permute-start.15
  112.5 22.2 %collective-permute-done.8.refs_5_ = f32[8,384]{1,0:T(8,128)S(1)} collective-permute-done((f32[8,384]{1,0:T(8,128)S(1)}, f32[8,384]{1,0:T(8,128)S(1)}, u32[]{:S(2)}, u32[]{:S(2)}) %collective-permute-start.8) | collective-permute-done | bytes 12320 | tf_op jit(solution)/shard_map/ppermute | solution.py:444
  136.5 8.6 %attend.6 = (f32[384,512]{1,0:T(8,128)S(1)}, bf16[384,512]{1,0:T(8,128)(2,1)S(1)}, bf16[384,512]{1,0:T(8,128)(2,1)}, f32[8,384]{1,0:T(8,128)S(1)}, f32[8,384]{1,0:T(8,128)S(1)}, /*index=5*/f32[8,384]{1,0:T(8,128)S(1)}) custom-call(s32[5]{0:T(128)S(1)} %copy-done.9, bf16[384,2048]{1,0:T(8,128)(2,1)S(1)} %copy-done, ...), custom_call_target="tpu_custom_call" | custom-call | flops 905969664 | bytes 4325376 | tf_op jit(solution)/shard_map/attend/pallas_call | solution.py:325
  145.7 1.3 collective-permute-start.23
  147.0 1.3 collective-permute-start.24
  148.3 5.8 %collective-permute-done.23.refs_5_ = f32[8,384]{1,0:T(8,128)S(1)} collective-permute-done((f32[8,384]{1,0:T(8,128)S(1)}, f32[8,384]{1,0:T(8,128)S(1)}, u32[]{:S(2)}, u32[]{:S(2)}) %collective-permute-start.23) | collective-permute-done | bytes 12320 | tf_op jit(solution)/shard_map/ppermute | solution.py:443
  154.1 1.3 collective-permute-start.14
  155.4 8.1 %collective-permute-done.24.refs_6_ = f32[8,384]{1,0:T(8,128)S(1)} collective-permute-done((f32[8,384]{1,0:T(8,128)S(1)}, f32[8,384]{1,0:T(8,128)S(1)}, u32[]{:S(2)}, u32[]{:S(2)}) %collective-permute-start.24) | collective-permute-done | bytes 12320 | tf_op jit(solution)/shard_map/ppermute | solution.py:444
  164.9 1.3 collective-permute-start.22
  166.2 8.6 %attend.7 = (f32[384,512]{1,0:T(8,128)S(1)}, bf16[384,512]{1,0:T(8,128)(2,1)}, bf16[384,512]{1,0:T(8,128)(2,1)S(1)}, f32[8,384]{1,0:T(8,128)S(1)}, f32[8,384]{1,0:T(8,128)}, /*index=5*/f32[8,384]{1,0:T(8,128)S(1)}) custom-call(s32[5]{0:T(128)S(1)} %copy-done.9, bf16[384,2048]{1,0:T(8,128)(2,1)S(1)} %copy-done, ...), custom_call_target="tpu_custom_call" | custom-call | flops 905969664 | bytes 4325376 | tf_op jit(solution)/shard_map/attend/pallas_call | solution.py:325
  176.3 1.3 collective-permute-start.29
  177.6 1.3 collective-permute-start.30
  178.9 1.3 collective-permute-start.31
  180.2 1.3 collective-permute-done.21.refs_2_
  182.9 4.4 %combine.4.refs_0_ = bf16[384,2048]{1,0:T(8,128)(2,1)} custom-call(s32[5]{0:T(128)} %pad_add_fusion.facts_ref, f32[384,512]{1,0:T(8,128)} %copy-done.3, bf16[384,512]{1,0:T(8,128)(2,1)} %copy-done.21, bf16[384,512]{1,0:T(8,128)(2,1)} %copy-done.22, f32[8,384]{1,0:T(8,128)} %copy-done.10, f32[8,384]{1,0:T(8,128)} %copy-done.23, f32[8,384]{1,0:T(8,128)} %copy-done.24), custom_call_target="tpu_custom_call" | custom-call | flops 3145728 | bytes 1966080 | tf_op jit(solution)/shard_map/combine/pallas_call | solution.py:388
  187.3 4.4 %combine.5.refs_0_ = bf16[384,2048]{1,0:T(8,128)(2,1)} custom-call(s32[5]{0:T(128)} %pad_add_fusion.facts_ref, bf16[384,2048]{1,0:T(8,128)(2,1)} %combine.4.refs_0_, f32[384,512]{1,0:T(8,128)} %copy-done.4, bf16[384,512]{1,0:T(8,128)(2,1)} %copy-done.16, bf16[384,512]{1,0:T(8,128)(2,1)} %copy-done.19, ...), custom_call_target="tpu_custom_call", output_to_operand_aliasing={{}: (1, {})} | custom-call | flops 3145728 | bytes 1966080 | tf_op jit(solution)/shard_map/combine/pallas_call | solution.py:388
  191.7 4.4 %combine.6.refs_0_ = bf16[384,2048]{1,0:T(8,128)(2,1)} custom-call(s32[5]{0:T(128)} %pad_add_fusion.facts_ref, bf16[384,2048]{1,0:T(8,128)(2,1)} %combine.5.refs_0_, f32[384,512]{1,0:T(8,128)} %copy-done.5, bf16[384,512]{1,0:T(8,128)(2,1)} %copy-done.17, bf16[384,512]{1,0:T(8,128)(2,1)} %collective-permute-done.22.refs_3_, ...), custom_call_target="tpu_custom_call", output_to_operand_aliasing={{}: (1, {})} | custom-call | flops 3145728 | bytes 1966080 | tf_op jit(solution)/shard_map/combine/pallas_call | solution.py:388
  196.1 2.2 %collective-permute-done.31.refs_5_ = f32[8,384]{1,0:T(8,128)S(1)} collective-permute-done((f32[8,384]{1,0:T(8,128)}, f32[8,384]{1,0:T(8,128)S(1)}, u32[]{:S(2)}, u32[]{:S(2)}) %collective-permute-start.31) | collective-permute-done | bytes 12320 | tf_op jit(solution)/shard_map/ppermute | solution.py:443
  198.4 9.1 %collective-permute-done.32.refs_6_ = f32[8,384]{1,0:T(8,128)S(1)} collective-permute-done((f32[8,384]{1,0:T(8,128)S(1)}, f32[8,384]{1,0:T(8,128)S(1)}, u32[]{:S(2)}, u32[]{:S(2)}) %collective-permute-start.32) | collective-permute-done | bytes 12320 | tf_op jit(solution)/shard_map/ppermute | solution.py:444
  208.4 4.4 %combine.7 = bf16[384,2048]{1,0:T(8,128)(2,1)} custom-call(s32[5]{0:T(128)} %pad_add_fusion.facts_ref, bf16[384,2048]{1,0:T(8,128)(2,1)} %combine.6.refs_0_, f32[384,512]{1,0:T(8,128)} %copy-done.6, bf16[384,512]{1,0:T(8,128)(2,1)} %copy-done.18, bf16[384,512]{1,0:T(8,128)(2,1)} %copy-done.20, f32[8,384]{1,0:T(8,128)} %copy-done.13, ...), custom_call_target="tpu_custom_call", output_to_operand_aliasing={{}: (1, {})} | custom-call | flops 3145728 | bytes 1966080 | tf_op jit(solution)/shard_map/combine/pallas_call | solution.py:388
  (99 shorter events, 16.7 us)
Async XLA Ops:
  2.9 9.4 %copy-start.1 = (bf16[384,2048]{1,0:T(8,128)(2,1)S(1)}, bf16[384,2048]{1,0:T(8,128)(2,1)}, u32[]{:S(2)}) copy-start(bf16[384,2048]{1,0:T(8,128)(2,1)} %own_k.7) | copy-start | bytes 4718596
  2.9 27.0 %collective-permute-start = (bf16[128,2048]{1,0:T(8,128)(2,1)}, bf16[128,2048]{1,0:T(8,128)(2,1)}, u32[]{:S(2)}, u32[]{:S(2)}) collective-permute-start(bf16[128,2048]{1,0:T(8,128)(2,1)} %multiply_convert_fusion), channel_id=1, source_target_pairs={{0,4},{4,8},{8,12},{1,5},{5,9},{9,13},{2,6},{6,10},{10,14},{3,7},{... | collective-permute-start | bytes 1572872 | tf_op jit(solution)/shard_map/ppermute | solution.py:17
  5.5 15.8 %copy-start.31 = (s32[4]{0:T(128)S(1)}, s32[4]{0:T(128)}, u32[]{:S(2)}) copy-start(s32[4]{0:T(128)} %param.15) | copy-start | bytes 52
  5.5 16.4 %collective-permute-start.1 = (bf16[384,512]{1,0:T(8,128)(2,1)}, bf16[384,512]{1,0:T(8,128)(2,1)S(1)}, u32[]{:S(2)}, u32[]{:S(2)}) collective-permute-start(bf16[384,512]{1,0:T(8,128)(2,1)} %get-tuple-element.61), channel_id=1, source_target_pairs={{8,4},{12,8},{9,5},{13,9},{10,6},{14,10},{11,7},{15,11},{24,20},{2... | collective-permute-start | bytes 1179656 | tf_op jit(solution)/shard_map/ppermute | solution.py:431
  10.2 18.3 %collective-permute-start.2 = (bf16[384,512]{1,0:T(8,128)(2,1)}, bf16[384,512]{1,0:T(8,128)(2,1)}, u32[]{:S(2)}, u32[]{:S(2)}) collective-permute-start(bf16[384,512]{1,0:T(8,128)(2,1)} %get-tuple-element.61), channel_id=1, source_target_pairs={{12,4},{13,5},{14,6},{15,7},{28,20},{29,21},{30,22},{31,23}} | collective-permute-start | bytes 1179656 | tf_op jit(solution)/shard_map/ppermute | solution.py:432
  13.5 33.7 %collective-permute-start.3 = (bf16[384,512]{1,0:T(8,128)(2,1)}, bf16[384,512]{1,0:T(8,128)(2,1)}, u32[]{:S(2)}, u32[]{:S(2)}) collective-permute-start(bf16[384,512]{1,0:T(8,128)(2,1)} %get-tuple-element.57), channel_id=1, source_target_pairs={{0,4},{1,5},{2,6},{3,7},{16,20},{17,21},{18,22},{19,23}} | collective-permute-start | bytes 1179656 | tf_op jit(solution)/shard_map/ppermute | solution.py:430
  14.9 37.6 %collective-permute-start.10 = (bf16[384,512]{1,0:T(8,128)(2,1)}, bf16[384,512]{1,0:T(8,128)(2,1)}, u32[]{:S(2)}, u32[]{:S(2)}) collective-permute-start(bf16[384,512]{1,0:T(8,128)(2,1)} %get-tuple-element.60), channel_id=1, source_target_pairs={{12,4},{13,5},{14,6},{15,7},{28,20},{29,21},{30,22},{31,23}} | collective-permute-start | bytes 1179656 | tf_op jit(solution)/shard_map/ppermute | solution.py:432
  22.6 32.2 %collective-permute-start.9 = (bf16[384,512]{1,0:T(8,128)(2,1)}, bf16[384,512]{1,0:T(8,128)(2,1)}, u32[]{:S(2)}, u32[]{:S(2)}) collective-permute-start(bf16[384,512]{1,0:T(8,128)(2,1)} %get-tuple-element.60), channel_id=1, source_target_pairs={{8,4},{12,8},{9,5},{13,9},{10,6},{14,10},{11,7},{15,11},{24,20},{2... | collective-permute-start | bytes 1179656 | tf_op jit(solution)/shard_map/ppermute | solution.py:431
  28.5 28.2 %collective-permute-start.11 = (bf16[384,512]{1,0:T(8,128)(2,1)}, bf16[384,512]{1,0:T(8,128)(2,1)}, u32[]{:S(2)}, u32[]{:S(2)}) collective-permute-start(bf16[384,512]{1,0:T(8,128)(2,1)} %get-tuple-element.56), channel_id=1, source_target_pairs={{0,4},{1,5},{2,6},{3,7},{16,20},{17,21},{18,22},{19,23}} | collective-permute-start | bytes 1179656 | tf_op jit(solution)/shard_map/ppermute | solution.py:430
  29.9 27.5 %collective-permute-start.17 = (bf16[384,512]{1,0:T(8,128)(2,1)}, bf16[384,512]{1,0:T(8,128)(2,1)S(1)}, u32[]{:S(2)}, u32[]{:S(2)}) collective-permute-start(bf16[384,512]{1,0:T(8,128)(2,1)} %get-tuple-element.59), channel_id=1, source_target_pairs={{8,4},{12,8},{9,5},{13,9},{10,6},{14,10},{11,7},{15,11},{24,20},{2... | collective-permute-start | bytes 1179656 | tf_op jit(solution)/shard_map/ppermute | solution.py:431
  47.2 15.1 %collective-permute-start.18 = (bf16[384,512]{1,0:T(8,128)(2,1)}, bf16[384,512]{1,0:T(8,128)(2,1)S(1)}, u32[]{:S(2)}, u32[]{:S(2)}) collective-permute-start(bf16[384,512]{1,0:T(8,128)(2,1)} %get-tuple-element.59), channel_id=1, source_target_pairs={{12,4},{13,5},{14,6},{15,7},{28,20},{29,21},{30,22},{31,23}} | collective-permute-start | bytes 1179656 | tf_op jit(solution)/shard_map/ppermute | solution.py:432
  52.4 15.1 %copy-start.15 = (bf16[384,512]{1,0:T(8,128)(2,1)S(1)}, bf16[384,512]{1,0:T(8,128)(2,1)}, u32[]{:S(2)}) copy-start(bf16[384,512]{1,0:T(8,128)(2,1)} %get-tuple-element.54) | copy-start | bytes 1179652
  52.5 19.6 %copy-start.2 = (bf16[384,2048]{1,0:T(8,128)(2,1)S(1)}, bf16[384,2048]{1,0:T(8,128)(2,1)}, u32[]{:S(2)}) copy-start(bf16[384,2048]{1,0:T(8,128)(2,1)} %hyena.1.own_v) | copy-start | bytes 4718596
  52.5 19.6 %copy-start.8 = (bf16[384,512]{1,0:T(8,128)(2,1)S(1)}, bf16[384,512]{1,0:T(8,128)(2,1)}, u32[]{:S(2)}) copy-start(bf16[384,512]{1,0:T(8,128)(2,1)} %copy-done.7) | copy-start | bytes 1179652
  52.5 19.6 %copy-start.9 = (s32[5]{0:T(128)S(1)}, s32[5]{0:T(128)}, u32[]{:S(2)}) copy-start(s32[5]{0:T(128)} %pad_add_fusion.facts_ref) | copy-start | bytes 64
  52.5 15.0 %collective-permute-start.19 = (bf16[384,512]{1,0:T(8,128)(2,1)}, bf16[384,512]{1,0:T(8,128)(2,1)S(1)}, u32[]{:S(2)}, u32[]{:S(2)}) collective-permute-start(bf16[384,512]{1,0:T(8,128)(2,1)} %get-tuple-element.55), channel_id=1, source_target_pairs={{0,4},{1,5},{2,6},{3,7},{16,20},{17,21},{18,22},{19,23}} | collective-permute-start | bytes 1179656 | tf_op jit(solution)/shard_map/ppermute | solution.py:430
  54.8 15.8 %collective-permute-start.25 = (bf16[384,512]{1,0:T(8,128)(2,1)S(1)}, bf16[384,512]{1,0:T(8,128)(2,1)S(1)}, u32[]{:S(2)}, u32[]{:S(2)}) collective-permute-start(bf16[384,512]{1,0:T(8,128)(2,1)S(1)} %copy-done.14), channel_id=1, source_target_pairs={{8,4},{12,8},{9,5},{13,9},{10,6},{14,10},{11,7},{15,11},{24,20},{2... | collective-permute-start | bytes 1179656 | tf_op jit(solution)/shard_map/ppermute | solution.py:431
  56.7 14.6 %collective-permute-start.4 = (bf16[384,512]{1,0:T(8,128)(2,1)S(1)}, bf16[384,512]{1,0:T(8,128)(2,1)S(1)}, u32[]{:S(2)}, u32[]{:S(2)}) collective-permute-start(bf16[384,512]{1,0:T(8,128)(2,1)S(1)} %get-tuple-element.53), channel_id=1, source_target_pairs={{0,4},{1,5},{2,6},{3,7},{16,20},{17,21},{18,22},{19,23}} | collective-permute-start | bytes 1179656 | tf_op jit(solution)/shard_map/ppermute | solution.py:433
  57.4 23.8 %collective-permute-start.12 = (bf16[384,512]{1,0:T(8,128)(2,1)S(1)}, bf16[384,512]{1,0:T(8,128)(2,1)S(1)}, u32[]{:S(2)}, u32[]{:S(2)}) collective-permute-start(bf16[384,512]{1,0:T(8,128)(2,1)S(1)} %get-tuple-element.52), channel_id=1, source_target_pairs={{0,4},{1,5},{2,6},{3,7},{16,20},{17,21},{18,22},{19,23}} | collective-permute-start | bytes 1179656 | tf_op jit(solution)/shard_map/ppermute | solution.py:433
  62.3 29.3 %collective-permute-start.26 = (bf16[384,512]{1,0:T(8,128)(2,1)S(1)}, bf16[384,512]{1,0:T(8,128)(2,1)S(1)}, u32[]{:S(2)}, u32[]{:S(2)}) collective-permute-start(bf16[384,512]{1,0:T(8,128)(2,1)S(1)} %copy-done.14), channel_id=1, source_target_pairs={{12,4},{13,5},{14,6},{15,7},{28,20},{29,21},{30,22},{31,23}} | collective-permute-start | bytes 1179656 | tf_op jit(solution)/shard_map/ppermute | solution.py:432
  67.5 25.4 %collective-permute-start.27 = (bf16[384,512]{1,0:T(8,128)(2,1)S(1)}, bf16[384,512]{1,0:T(8,128)(2,1)S(1)}, u32[]{:S(2)}, u32[]{:S(2)}) collective-permute-start(bf16[384,512]{1,0:T(8,128)(2,1)S(1)} %copy-done.15), channel_id=1, source_target_pairs={{0,4},{1,5},{2,6},{3,7},{16,20},{17,21},{18,22},{19,23}} | collective-permute-start | bytes 1179656 | tf_op jit(solution)/shard_map/ppermute | solution.py:430
  70.6 23.6 %collective-permute-start.20 = (bf16[384,512]{1,0:T(8,128)(2,1)S(1)}, bf16[384,512]{1,0:T(8,128)(2,1)S(1)}, u32[]{:S(2)}, u32[]{:S(2)}) collective-permute-start(bf16[384,512]{1,0:T(8,128)(2,1)S(1)} %get-tuple-element.51), channel_id=1, source_target_pairs={{0,4},{1,5},{2,6},{3,7},{16,20},{17,21},{18,22},{19,23}} | collective-permute-start | bytes 1179656 | tf_op jit(solution)/shard_map/ppermute | solution.py:433
  71.3 24.2 %collective-permute-start.28 = (bf16[384,512]{1,0:T(8,128)(2,1)S(1)}, bf16[384,512]{1,0:T(8,128)(2,1)S(1)}, u32[]{:S(2)}, u32[]{:S(2)}) collective-permute-start(bf16[384,512]{1,0:T(8,128)(2,1)S(1)} %get-tuple-element.50), channel_id=1, source_target_pairs={{0,4},{1,5},{2,6},{3,7},{16,20},{17,21},{18,22},{19,23}} | collective-permute-start | bytes 1179656 | tf_op jit(solution)/shard_map/ppermute | solution.py:433
  81.2 9.8 %copy-start.3 = (f32[384,512]{1,0:T(8,128)}, f32[384,512]{1,0:T(8,128)S(1)}, u32[]{:S(2)}) copy-start(f32[384,512]{1,0:T(8,128)S(1)} %get-tuple-element.26.refs_0_) | copy-start | bytes 2359300
  81.2 83.6 %collective-permute-start.5 = (bf16[384,512]{1,0:T(8,128)(2,1)S(1)}, bf16[384,512]{1,0:T(8,128)(2,1)S(1)}, u32[]{:S(2)}, u32[]{:S(2)}) collective-permute-start(bf16[384,512]{1,0:T(8,128)(2,1)S(1)} %get-tuple-element.27), channel_id=1, source_target_pairs={{4,8},{8,12},{5,9},{9,13},{6,10},{10,14},{7,11},{11,15},{20,24},{2... | collective-permute-start | bytes 1179656 | tf_op jit(solution)/shard_map/ppermute | solution.py:440
  91.6 53.5 %copy-start.4 = (f32[384,512]{1,0:T(8,128)}, f32[384,512]{1,0:T(8,128)S(1)}, u32[]{:S(2)}) copy-start(f32[384,512]{1,0:T(8,128)S(1)} %get-tuple-element.32.refs_1_) | copy-start | bytes 2359300
  91.6 84.7 %collective-permute-start.6 = (bf16[384,512]{1,0:T(8,128)(2,1)S(1)}, bf16[384,512]{1,0:T(8,128)(2,1)S(1)}, u32[]{:S(2)}, u32[]{:S(2)}) collective-permute-start(bf16[384,512]{1,0:T(8,128)(2,1)S(1)} %get-tuple-element.28), channel_id=1, source_target_pairs={{4,12},{5,13},{6,14},{7,15},{20,28},{21,29},{22,30},{23,31}} | collective-permute-start | bytes 1179656 | tf_op jit(solution)/shard_map/ppermute | solution.py:441
  92.9 84.7 %collective-permute-start.13 = (bf16[384,512]{1,0:T(8,128)(2,1)S(1)}, bf16[384,512]{1,0:T(8,128)(2,1)S(1)}, u32[]{:S(2)}, u32[]{:S(2)}) collective-permute-start(bf16[384,512]{1,0:T(8,128)(2,1)S(1)} %get-tuple-element.33), channel_id=1, source_target_pairs={{4,8},{8,12},{5,9},{9,13},{6,10},{10,14},{7,11},{11,15},{20,24},{2... | collective-permute-start | bytes 1179656 | tf_op jit(solution)/shard_map/ppermute | solution.py:440
  94.2 16.9 %collective-permute-start.7 = (f32[8,384]{1,0:T(8,128)S(1)}, f32[8,384]{1,0:T(8,128)S(1)}, u32[]{:S(2)}, u32[]{:S(2)}) collective-permute-start(f32[8,384]{1,0:T(8,128)S(1)} %get-tuple-element.30), channel_id=1, source_target_pairs={{4,8},{8,12},{5,9},{9,13},{6,10},{10,14},{7,11},{11,15},{20,24},{2... | collective-permute-start | bytes 36872 | tf_op jit(solution)/shard_map/ppermute | solution.py:443
  95.5 39.1 %collective-permute-start.8 = (f32[8,384]{1,0:T(8,128)S(1)}, f32[8,384]{1,0:T(8,128)S(1)}, u32[]{:S(2)}, u32[]{:S(2)}) collective-permute-start(f32[8,384]{1,0:T(8,128)S(1)} %get-tuple-element.31), channel_id=1, source_target_pairs={{4,12},{5,13},{6,14},{7,15},{20,28},{21,29},{22,30},{23,31}} | collective-permute-start | bytes 36872 | tf_op jit(solution)/shard_map/ppermute | solution.py:444
  111.2 23.5 %copy-start.23 = (f32[8,384]{1,0:T(8,128)}, f32[8,384]{1,0:T(8,128)S(1)}, u32[]{:S(2)}) copy-start(f32[8,384]{1,0:T(8,128)S(1)} %collective-permute-done.7.refs_4_) | copy-start | bytes 36868
  111.2 34.5 %collective-permute-start.15 = (f32[8,384]{1,0:T(8,128)S(1)}, f32[8,384]{1,0:T(8,128)S(1)}, u32[]{:S(2)}, u32[]{:S(2)}) collective-permute-start(f32[8,384]{1,0:T(8,128)S(1)} %get-tuple-element.36), channel_id=1, source_target_pairs={{4,8},{8,12},{5,9},{9,13},{6,10},{10,14},{7,11},{11,15},{20,24},{2... | collective-permute-start | bytes 36872 | tf_op jit(solution)/shard_map/ppermute | solution.py:443
  135.2 11.8 %collective-permute-start.16 = (f32[8,384]{1,0:T(8,128)S(1)}, f32[8,384]{1,0:T(8,128)S(1)}, u32[]{:S(2)}, u32[]{:S(2)}) collective-permute-start(f32[8,384]{1,0:T(8,128)S(1)} %get-tuple-element.37), channel_id=1, source_target_pairs={{4,12},{5,13},{6,14},{7,15},{20,28},{21,29},{22,30},{23,31}} | collective-permute-start | bytes 36872 | tf_op jit(solution)/shard_map/ppermute | solution.py:444
  145.7 29.1 %copy-start.5 = (f32[384,512]{1,0:T(8,128)}, f32[384,512]{1,0:T(8,128)S(1)}, u32[]{:S(2)}) copy-start(f32[384,512]{1,0:T(8,128)S(1)} %get-tuple-element.38.refs_1_) | copy-start | bytes 2359300
  145.7 19.2 %copy-start.25 = (f32[8,384]{1,0:T(8,128)}, f32[8,384]{1,0:T(8,128)S(1)}, u32[]{:S(2)}) copy-start(f32[8,384]{1,0:T(8,128)S(1)} %collective-permute-done.15.refs_5_) | copy-start | bytes 36868
  145.7 8.4 %collective-permute-start.23 = (f32[8,384]{1,0:T(8,128)S(1)}, f32[8,384]{1,0:T(8,128)S(1)}, u32[]{:S(2)}, u32[]{:S(2)}) collective-permute-start(f32[8,384]{1,0:T(8,128)S(1)} %get-tuple-element.42), channel_id=1, source_target_pairs={{4,8},{8,12},{5,9},{9,13},{6,10},{10,14},{7,11},{11,15},{20,24},{2... | collective-permute-start | bytes 36872 | tf_op jit(solution)/shard_map/ppermute | solution.py:443
  147.0 17.9 %copy-start.26 = (f32[8,384]{1,0:T(8,128)}, f32[8,384]{1,0:T(8,128)S(1)}, u32[]{:S(2)}) copy-start(f32[8,384]{1,0:T(8,128)S(1)} %collective-permute-done.16.refs_6_) | copy-start | bytes 36868
  147.0 16.5 %collective-permute-start.24 = (f32[8,384]{1,0:T(8,128)S(1)}, f32[8,384]{1,0:T(8,128)S(1)}, u32[]{:S(2)}, u32[]{:S(2)}) collective-permute-start(f32[8,384]{1,0:T(8,128)S(1)} %get-tuple-element.43), channel_id=1, source_target_pairs={{4,12},{5,13},{6,14},{7,15},{20,28},{21,29},{22,30},{23,31}} | collective-permute-start | bytes 36872 | tf_op jit(solution)/shard_map/ppermute | solution.py:444
  154.1 10.7 %copy-start.27 = (f32[8,384]{1,0:T(8,128)}, f32[8,384]{1,0:T(8,128)S(1)}, u32[]{:S(2)}) copy-start(f32[8,384]{1,0:T(8,128)S(1)} %collective-permute-done.23.refs_5_) | copy-start | bytes 36868
  154.1 24.8 %collective-permute-start.14 = (bf16[384,512]{1,0:T(8,128)(2,1)S(1)}, bf16[384,512]{1,0:T(8,128)(2,1)S(1)}, u32[]{:S(2)}, u32[]{:S(2)}) collective-permute-start(bf16[384,512]{1,0:T(8,128)(2,1)S(1)} %get-tuple-element.34), channel_id=1, source_target_pairs={{4,12},{5,13},{6,14},{7,15},{20,28},{21,29},{22,30},{23,31}} | collective-permute-start | bytes 1179656 | tf_op jit(solution)/shard_map/ppermute | solution.py:441
  163.5 18.0 %collective-permute-start.21 = (bf16[384,512]{1,0:T(8,128)(2,1)S(1)}, bf16[384,512]{1,0:T(8,128)(2,1)S(1)}, u32[]{:S(2)}, u32[]{:S(2)}) collective-permute-start(bf16[384,512]{1,0:T(8,128)(2,1)S(1)} %get-tuple-element.39), channel_id=1, source_target_pairs={{4,8},{8,12},{5,9},{9,13},{6,10},{10,14},{7,11},{11,15},{20,24},{2... | collective-permute-start | bytes 1179656 | tf_op jit(solution)/shard_map/ppermute | solution.py:440
  164.8 9.9 %copy-start.21 = (bf16[384,512]{1,0:T(8,128)(2,1)}, bf16[384,512]{1,0:T(8,128)(2,1)S(1)}, u32[]{:S(2)}) copy-start(bf16[384,512]{1,0:T(8,128)(2,1)S(1)} %collective-permute-done.5.refs_1_) | copy-start | bytes 1179652
  164.9 26.8 %collective-permute-start.22 = (bf16[384,512]{1,0:T(8,128)(2,1)}, bf16[384,512]{1,0:T(8,128)(2,1)}, u32[]{:S(2)}, u32[]{:S(2)}) collective-permute-start(bf16[384,512]{1,0:T(8,128)(2,1)} %get-tuple-element.40), channel_id=1, source_target_pairs={{4,12},{5,13},{6,14},{7,15},{20,28},{21,29},{22,30},{23,31}} | collective-permute-start | bytes 1179656 | tf_op jit(solution)/shard_map/ppermute | solution.py:441
  176.3 31.2 %collective-permute-start.29 = (bf16[384,512]{1,0:T(8,128)(2,1)}, bf16[384,512]{1,0:T(8,128)(2,1)S(1)}, u32[]{:S(2)}, u32[]{:S(2)}) collective-permute-start(bf16[384,512]{1,0:T(8,128)(2,1)} %get-tuple-element.45), channel_id=1, source_target_pairs={{4,8},{8,12},{5,9},{9,13},{6,10},{10,14},{7,11},{11,15},{20,24},{2... | collective-permute-start | bytes 1179656 | tf_op jit(solution)/shard_map/ppermute | solution.py:440
  177.6 29.9 %collective-permute-start.30 = (bf16[384,512]{1,0:T(8,128)(2,1)S(1)}, bf16[384,512]{1,0:T(8,128)(2,1)S(1)}, u32[]{:S(2)}, u32[]{:S(2)}) collective-permute-start(bf16[384,512]{1,0:T(8,128)(2,1)S(1)} %get-tuple-element.46), channel_id=1, source_target_pairs={{4,12},{5,13},{6,14},{7,15},{20,28},{21,29},{22,30},{23,31}} | collective-permute-start | bytes 1179656 | tf_op jit(solution)/shard_map/ppermute | solution.py:441
  178.9 19.4 %collective-permute-start.31 = (f32[8,384]{1,0:T(8,128)}, f32[8,384]{1,0:T(8,128)S(1)}, u32[]{:S(2)}, u32[]{:S(2)}) collective-permute-start(f32[8,384]{1,0:T(8,128)} %get-tuple-element.48), channel_id=1, source_target_pairs={{4,8},{8,12},{5,9},{9,13},{6,10},{10,14},{7,11},{11,15},{20,24},{2... | collective-permute-start | bytes 36872 | tf_op jit(solution)/shard_map/ppermute | solution.py:443
  181.6 25.9 %collective-permute-start.32 = (f32[8,384]{1,0:T(8,128)S(1)}, f32[8,384]{1,0:T(8,128)S(1)}, u32[]{:S(2)}, u32[]{:S(2)}) collective-permute-start(f32[8,384]{1,0:T(8,128)S(1)} %get-tuple-element.49), channel_id=1, source_target_pairs={{4,12},{5,13},{6,14},{7,15},{20,28},{21,29},{22,30},{23,31}} | collective-permute-start | bytes 36872 | tf_op jit(solution)/shard_map/ppermute | solution.py:444
  198.4 9.2 %copy-start.29 = (f32[8,384]{1,0:T(8,128)}, f32[8,384]{1,0:T(8,128)S(1)}, u32[]{:S(2)}) copy-start(f32[8,384]{1,0:T(8,128)S(1)} %collective-permute-done.31.refs_5_) | copy-start | bytes 36868
  (17 other events, 31.3 us)

commit v3 on v2

--- a/solution.py
+++ b/solution.py
@@ -140,6 +140,7 @@
 NEVER = -1e29
 BLOCK = 128
 CHUNKS = 4
+AHEAD = 2
 EXPONENT = math.log2(math.e) / math.sqrt(HEAD_DIM)
 
 
@@ -152,7 +153,7 @@
 
 
 def hyena_kernel(genomes, facts_ref, query_ref, key_ref, value_ref, halo_ref, taps_ref, gain_ref,
-                 mix_ref, extended, masks):
+                 mix_ref, extended, masks, bands):
     rows = key_ref.shape[0]
     blocks = rows // BLOCK
     groups = taps_ref.shape[0]
@@ -175,17 +176,21 @@
     extended[:BLOCK] = halo_ref[...]
     extended[BLOCK:] = product
     lane_group = lax.broadcasted_iota(jnp.int32, (BLOCK, BLOCK), 1) // group_width
-    totals = [jnp.zeros((BLOCK, BLOCK), jnp.float32) for b in range(blocks)]
     for g in range(groups):
         row = jnp.broadcast_to(taps_ref[g : g + 1, :], (BLOCK, BLOCK))
         turned = pltpu.roll(row, 0, 1, stride=1, stride_axis=0).astype(jnp.bfloat16)
         both = jnp.concatenate([turned, turned], axis=1)
         for b in range(blocks):
-            band = both * masks[b]
-            part = jnp.dot(
-                band, extended[b * BLOCK : (b + 2) * BLOCK], preferred_element_type=jnp.float32
-            )
-            totals[b] = jnp.where(lane_group == g, part, totals[b])
+            bands[b, g * BLOCK : (g + 1) * BLOCK] = both * masks[b]
+    totals = []
+    for b in range(blocks):
+        parts = jnp.dot(
+            bands[b], extended[b * BLOCK : (b + 2) * BLOCK], preferred_element_type=jnp.float32
+        )
+        picked = parts[:BLOCK]
+        for g in range(1, groups):
+            picked = jnp.where(lane_group == g, parts[g * BLOCK : (g + 1) * BLOCK], picked)
+        totals.append(picked)
     for b in range(blocks):
         here = slice(b * BLOCK, (b + 1) * BLOCK)
         wide = extended[(b + 1) * BLOCK : (b + 2) * BLOCK].astype(jnp.float32)
@@ -216,6 +221,7 @@
             scratch_shapes=[
                 pltpu.VMEM((rows + BLOCK, BLOCK), jnp.bfloat16),
                 pltpu.VMEM((rows // BLOCK, BLOCK, 2 * BLOCK), jnp.bfloat16),
+                pltpu.VMEM((rows // BLOCK, groups * BLOCK, 2 * BLOCK), jnp.bfloat16),
             ],
         ),
         cost_estimate=pl.CostEstimate(
@@ -241,12 +247,24 @@
     return mixed[:, :HEAD_DIM] / safe, log
 
 
+def pieces_of(log):
+    high = log.astype(jnp.bfloat16)
+    rest = log - high.astype(jnp.float32)
+    middle = rest.astype(jnp.bfloat16)
+    low = (rest - middle.astype(jnp.float32)).astype(jnp.bfloat16)
+    return jnp.concatenate([high, middle, low, jnp.zeros_like(low)])
+
+
+def joined(pieces):
+    wide = pieces.astype(jnp.float32)
+    return wide[:8] + wide[8:16] + wide[16:24]
+
+
 def attend_kernel(genomes, facts_ref, own_q, next_q, last_q, own_k, own_v, far_k, far_v,
-                  own_o, next_o, last_o, own_l, next_l, last_l, queries, keys, values, bias,
-                  mixed, logs):
-    rows = own_q.shape[0]
+                  own_o, next_o, last_o, own_l, queries, keys, values, bias, mixed, logs):
+    rows, width = own_q.shape
+    heads = width // HEAD_DIM
     per_shard = rows // BLOCK
-    head = pl.program_id(0)
     shard = facts_ref[genomes]
     own_first = shard * rows
     base = own_first - rows
@@ -256,27 +274,28 @@
     def rows_of(step):
         return pl.ds(pl.multiple_of(step * BLOCK, BLOCK), BLOCK)
 
-    @pl.when(head == 0)
-    def _():
-        values[:, HEAD_DIM:] = jnp.ones((2 * rows, HEAD_DIM), jnp.bfloat16)
-        logs[...] = jnp.full_like(logs, NEVER)
-
-        def fill(step, nothing):
-            query_pos = own_first + step * BLOCK + lax.broadcasted_iota(jnp.int32, (BLOCK, 1), 0)
-            begin = jnp.maximum(begin_of(query_pos, facts_ref, genomes), limit)
-            key_pos = base + lax.broadcasted_iota(jnp.int32, (BLOCK, 2 * rows), 1)
-            visible = (key_pos >= begin) & (key_pos <= query_pos)
-            bias[rows_of(step), :] = jnp.where(visible, 0.0, 10 * NEVER)
-            return nothing
-
-        lax.fori_loop(0, steps, fill, 0)
-
+    logs[...] = jnp.full_like(logs, NEVER)
+
+    def fill(step, nothing):
+        query_pos = own_first + step * BLOCK + lax.broadcasted_iota(jnp.int32, (BLOCK, 1), 0)
+        begin = jnp.maximum(begin_of(query_pos, facts_ref, genomes), limit)
+        key_pos = base + lax.broadcasted_iota(jnp.int32, (BLOCK, 2 * rows), 1)
+        visible = (key_pos >= begin) & (key_pos <= query_pos)
+        bias[rows_of(step), :] = jnp.where(visible, 0.0, 10 * NEVER)
+        return nothing
+
+    lax.fori_loop(0, steps, fill, 0)
     for slot, ref in enumerate((own_q, next_q, last_q)):
         queries[slot * rows : (slot + 1) * rows] = ref[...]
     for slot, (k_ref, v_ref) in enumerate(((far_k, far_v), (own_k, own_v))):
         here = slice(slot * rows, (slot + 1) * rows)
         keys[here] = k_ref[...]
-        values[here, :HEAD_DIM] = v_ref[...]
+        for head in range(heads):
+            first = 2 * head * HEAD_DIM
+            values[here, first : first + HEAD_DIM] = v_ref[:, head * HEAD_DIM : (head + 1) * HEAD_DIM]
+            values[here, first + HEAD_DIM : first + 2 * HEAD_DIM] = jnp.ones(
+                (rows, HEAD_DIM), jnp.bfloat16
+            )
 
     def one_step(step, nothing):
         query_first = own_first + step * BLOCK
@@ -290,59 +309,71 @@
 
         @pl.when(count <= 0)
         def _():
-            mixed[rows_of(step), :] = jnp.zeros((BLOCK, HEAD_DIM), jnp.float32)
+            mixed[rows_of(step), :] = jnp.zeros((BLOCK, width), jnp.float32)
 
         for blocks in range(1, 2 * per_shard + 1):
 
             @pl.when(count == blocks)
             def _():
                 span = pl.ds(pl.multiple_of(first * BLOCK, BLOCK), blocks * BLOCK)
-                out, log = attend_block(
-                    queries[rows_of(step), :], keys[span, :], values[span, :], bias[rows_of(step), span]
-                )
-                mixed[rows_of(step), :] = out
+                mask = bias[rows_of(step), span]
                 lane = lax.broadcasted_iota(jnp.int32, (BLOCK, BLOCK), 1)
-                logs[rows_of(step), :] = jnp.where(lane == head, log, logs[rows_of(step), :])
+                gathered = jnp.full((BLOCK, BLOCK), NEVER, jnp.float32)
+                for head in range(heads):
+                    here = slice(head * HEAD_DIM, (head + 1) * HEAD_DIM)
+                    both = slice(2 * head * HEAD_DIM, 2 * (head + 1) * HEAD_DIM)
+                    out, log = attend_block(
+                        queries[rows_of(step), here], keys[span, here], values[span, both], mask
+                    )
+                    mixed[rows_of(step), here] = out
+                    gathered = jnp.where(lane == head, log, gathered)
+                logs[rows_of(step), :] = gathered
 
         return nothing
 
     lax.fori_loop(0, steps, one_step, 0)
-    for slot, ref in enumerate((own_o, next_o, last_o)):
-        ref[...] = mixed[slot * rows : (slot + 1) * rows].astype(ref.dtype)
-
-    @pl.when(head == pl.num_programs(0) - 1)
-    def _():
-        for slot, ref in enumerate((own_l, next_l, last_l)):
-            ref[...] = jnp.transpose(logs[slot * rows : (slot + 1) * rows])[:8]
+    own_o[...] = mixed[:rows]
+    own_l[...] = jnp.transpose(logs[:rows])[:8]
+    for slot, ref, used in ((1, next_o, (shard == 1) | (shard == 2)), (2, last_o, shard == 1)):
+
+        @pl.when(used)
+        def _():
+            here = slice(slot * rows, (slot + 1) * rows)
+            ref[:rows] = mixed[here].astype(ref.dtype)
+            ref[rows:, :rows] = pieces_of(jnp.transpose(logs[here])[:8])
+            ref[rows:, rows:] = jnp.zeros((32, width - rows), ref.dtype)
+
+        @pl.when(jnp.logical_not(used))
+        def _():
+            ref[...] = jnp.zeros_like(ref)
 
 
 def attend(facts, genomes, chunk, heads, own_q, next_q, last_q, own_k, own_v, far_k, far_v):
     rows = own_q.shape[0]
-    whole = pl.BlockSpec((rows, HEAD_DIM), lambda h, facts_ref: (0, chunk * heads + h))
-    piece = pl.BlockSpec((rows, HEAD_DIM), lambda h, facts_ref: (0, h))
+    width = heads * HEAD_DIM
+    whole = pl.BlockSpec((rows, width), lambda h, facts_ref: (0, chunk))
+    piece = pl.BlockSpec((rows, width), lambda h, facts_ref: (0, 0))
+    sent = pl.BlockSpec((rows + 32, width), lambda h, facts_ref: (0, 0))
     logs = pl.BlockSpec((8, rows), lambda h, facts_ref: (0, 0))
-    width = heads * HEAD_DIM
     return pl.pallas_call(
         partial(attend_kernel, genomes),
         out_shape=(
             jax.ShapeDtypeStruct((rows, width), jnp.float32),
-            jax.ShapeDtypeStruct((rows, width), jnp.bfloat16),
-            jax.ShapeDtypeStruct((rows, width), jnp.bfloat16),
-            jax.ShapeDtypeStruct((8, rows), jnp.float32),
-            jax.ShapeDtypeStruct((8, rows), jnp.float32),
+            jax.ShapeDtypeStruct((rows + 32, width), jnp.bfloat16),
+            jax.ShapeDtypeStruct((rows + 32, width), jnp.bfloat16),
             jax.ShapeDtypeStruct((8, rows), jnp.float32),
         ),
         grid_spec=pltpu.PrefetchScalarGridSpec(
             num_scalar_prefetch=1,
-            grid=(heads,),
+            grid=(1,),
             in_specs=[whole, piece, piece, whole, whole, piece, piece],
-            out_specs=[piece, piece, piece, logs, logs, logs],
+            out_specs=[piece, sent, sent, logs],
             scratch_shapes=[
-                pltpu.VMEM((3 * rows, HEAD_DIM), jnp.bfloat16),
-                pltpu.VMEM((2 * rows, HEAD_DIM), jnp.bfloat16),
-                pltpu.VMEM((2 * rows, 2 * HEAD_DIM), jnp.bfloat16),
+                pltpu.VMEM((3 * rows, width), jnp.bfloat16),
+                pltpu.VMEM((2 * rows, width), jnp.bfloat16),
+                pltpu.VMEM((2 * rows, 2 * width), jnp.bfloat16),
                 pltpu.VMEM((3 * rows, 2 * rows), jnp.float32),
-                pltpu.VMEM((3 * rows, HEAD_DIM), jnp.float32),
+                pltpu.VMEM((3 * rows, width), jnp.float32),
                 pltpu.VMEM((3 * rows, BLOCK), jnp.float32),
             ],
         ),
@@ -356,52 +387,53 @@
     )(facts, own_q, next_q, last_q, own_k, own_v, far_k, far_v)
 
 
-def combine_kernel(genomes, facts_ref, *refs):
-    own_o, near_o, far_o, own_l, near_l, far_l = refs[-7:-1]
+def combine_kernel(genomes, heads, facts_ref, *refs):
     out_ref = refs[-1]
-    width = own_o.shape[1]
+    width = heads * HEAD_DIM
     shard = facts_ref[genomes]
-    own = own_l[...]
-    near = jnp.where(shard >= 2, near_l[...], NEVER)
-    far = jnp.where(shard == 3, far_l[...], NEVER)
-    highest = jnp.maximum(own, jnp.maximum(near, far))
-    shares = [jnp.exp2(log - highest) for log in (own, near, far)]
-    whole = shares[0] + shares[1] + shares[2]
-    columns = [
-        jnp.transpose(jnp.concatenate([share / whole] + [jnp.zeros((BLOCK - 8, BLOCK), jnp.float32)]))
-        for share in shares
-    ]
-    for head in range(width // HEAD_DIM):
-        here = slice(head * HEAD_DIM, (head + 1) * HEAD_DIM)
-        mixed = columns[0][:, head : head + 1] * own_o[:, here]
-        for column, ref in ((columns[1], near_o), (columns[2], far_o)):
-            mixed += column[:, head : head + 1] * ref[:, here].astype(jnp.float32)
-        out_ref[:, here] = mixed.astype(out_ref.dtype)
-
-
-def combine(facts, genomes, chunk, heads, channels, earlier, *pieces):
-    rows = pieces[0].shape[0]
-    width = heads * HEAD_DIM
+    for chunk in range(CHUNKS):
+        own_o, near_o, far_o, own_l, near_l, far_l = refs[6 * chunk : 6 * chunk + 6]
+        own = own_l[...]
+        near = jnp.where(shard >= 2, joined(near_l[...]), NEVER)
+        far = jnp.where(shard == 3, joined(far_l[...]), NEVER)
+        highest = jnp.maximum(own, jnp.maximum(near, far))
+        shares = [jnp.exp2(log - highest) for log in (own, near, far)]
+        whole = shares[0] + shares[1] + shares[2]
+        columns = [
+            jnp.transpose(
+                jnp.concatenate([share / whole, jnp.zeros((BLOCK - 8, BLOCK), jnp.float32)])
+            )
+            for share in shares
+        ]
+        for head in range(heads):
+            here = slice(head * HEAD_DIM, (head + 1) * HEAD_DIM)
+            mixed = columns[0][:, head : head + 1] * own_o[:, here]
+            for column, ref in ((columns[1], near_o), (columns[2], far_o)):
+                mixed += column[:, head : head + 1] * ref[:, here].astype(jnp.float32)
+            first = chunk * width + head * HEAD_DIM
+            out_ref[:, first : first + HEAD_DIM] = mixed.astype(out_ref.dtype)
+
+
+def combine(facts, genomes, heads, channels, parts):
+    rows, width = parts[0][0].shape
     piece = pl.BlockSpec((BLOCK, width), lambda r, facts_ref: (r, 0))
-    logs = pl.BlockSpec((8, BLOCK), lambda r, facts_ref: (0, r))
-    held = () if earlier is None else (earlier,)
+    own = pl.BlockSpec((8, BLOCK), lambda r, facts_ref: (0, r))
+    logs = pl.BlockSpec((32, BLOCK), lambda r, facts_ref: (rows // 32, r))
+    operands = [x for o, near, far, l in parts for x in (o, near, far, l, near, far)]
     return pl.pallas_call(
-        partial(combine_kernel, genomes),
+        partial(combine_kernel, genomes, heads),
         out_shape=jax.ShapeDtypeStruct((rows, channels), jnp.bfloat16),
         grid_spec=pltpu.PrefetchScalarGridSpec(
             num_scalar_prefetch=1,
             grid=(rows // BLOCK,),
-            in_specs=[pl.BlockSpec(memory_space=pl.ANY)] * len(held) + [piece] * 3 + [logs] * 3,
-            out_specs=pl.BlockSpec((BLOCK, width), lambda r, facts_ref: (r, chunk)),
-        ),
-        input_output_aliases={1: 0} if held else {},
+            in_specs=[piece, piece, piece, own, logs, logs] * CHUNKS,
+            out_specs=pl.BlockSpec((BLOCK, channels), lambda r, facts_ref: (r, 0)),
+        ),
         cost_estimate=pl.CostEstimate(
-            flops=rows * heads * HEAD_DIM * 16,
-            bytes_accessed=rows * heads * HEAD_DIM * 10,
-            transcendentals=0,
+            flops=rows * channels * 16, bytes_accessed=rows * channels * 10, transcendentals=0
         ),
         name="combine",
-    )(facts, *held, *pieces)
+    )(facts, *operands)
 
 
 def balanced_plan(
@@ -422,31 +454,31 @@
     )
     heads = channels // HEAD_DIM // CHUNKS
     width = heads * HEAD_DIM
-    attended = None
     parts = []
     for chunk in range(CHUNKS):
         here = slice(chunk * width, (chunk + 1) * width)
-        queries = attn_query[:, here]
-        far_k = lax.ppermute(attn_key[:, here], "ctx", [(0, 1)])
-        next_q = lax.ppermute(queries, "ctx", [(2, 1), (3, 2)])
-        last_q = lax.ppermute(queries, "ctx", [(3, 1)])
-        far_v = lax.ppermute(mix[:, here], "ctx", [(0, 1)])
-        own_o, next_o, last_o, own_l, next_l, last_l = attend(
-            facts, genomes, chunk, heads, attn_query, next_q, last_q, attn_key, mix, far_k, far_v
-        )
+        pieces = (attn_key[:, here], attn_query[:, here], mix[:, here])
+        if chunk >= AHEAD:
+            pieces, parts[chunk - AHEAD] = lax.optimization_barrier((pieces, parts[chunk - AHEAD]))
+        far_k = lax.ppermute(pieces[0], "ctx", [(0, 1)])
+        next_q = lax.ppermute(pieces[1], "ctx", [(2, 1), (3, 2)])
+        last_q = lax.ppermute(pieces[1], "ctx", [(3, 1)])
+        far_v = lax.ppermute(pieces[2], "ctx", [(0, 1)])
         parts.append(
-            (
-                own_o,
-                lax.ppermute(next_o, "ctx", [(1, 2), (2, 3)]),
-                lax.ppermute(last_o, "ctx", [(1, 3)]),
-                own_l,
-                lax.ppermute(next_l, "ctx", [(1, 2), (2, 3)]),
-                lax.ppermute(last_l, "ctx", [(1, 3)]),
+            attend(
+                facts, genomes, chunk, heads, attn_query, next_q, last_q, attn_key, mix, far_k, far_v
             )
         )
-    for chunk in range(CHUNKS):
-        attended = combine(facts, genomes, chunk, heads, channels, attended, *parts[chunk])
-    return (mix, attended)
+    returned = [
+        (
+            own_o,
+            lax.ppermute(next_o, "ctx", [(1, 2), (2, 3)]),
+            lax.ppermute(last_o, "ctx", [(1, 3)]),
+            own_l,
+        )
+        for own_o, next_o, last_o, own_l in parts
+    ]
+    return (mix, combine(facts, genomes, heads, channels, returned))
 
 
 def solution(mesh):

time: 212 us -> 182 us (0.86); the launches traced: 213 us -> 180 us
  Pallas kernels: 67.8 us -> 42.3 us
  waiting for transfers between devices: 72.5 us -> 66.5 us
  local copies, waits for them, and re-layouts: 12.3 us -> 9.81 us
    ppermute x24 -> x16, waiting for transfers between devices: 71.2 us -> 15.3 us  [the longest x4 14.2 us: balanced_plan(): next_q = lax.ppermute(pieces[1], 'ctx', [(2, 1), (3, 2)])]
    ppermute x4, waiting for transfers between devices: 0.01 us -> 42 us  [balanced_plan(): lax.ppermute(last_o, 'ctx', [(1, 3)])]
    pallas_call x4, Pallas kernels: 34.2 us -> 19 us  [attend(): pl.pallas_call(partial(attend_kernel, genomes), out_shape=(jax.ShapeDtype...]
    pallas_call x4 -> x1, Pallas kernels: 17.6 us -> 7.33 us  [combine(): pl.pallas_call(partial(combine_kernel, genomes, heads), out_shape=jax.Sha...]
    ppermute x4, waiting for transfers between devices: 1.33 us -> 9.25 us  [balanced_plan(): lax.ppermute(next_o, 'ctx', [(1, 2), (2, 3)])]
    unnamed x64 -> x54, local copies, waits for them, and re-layouts: 5.56 us -> 2.88 us
    ppermute x24 -> x16, starting transfers between devices: 42.9 us -> 44.5 us  [the longest x4 31.8 us: balanced_plan(): last_q = lax.ppermute(pieces[1], 'ctx', [(3, 1)])]
  transfers between devices with their start and end apart: 33 -> 25, of which waited for: 10 -> 11; matrix products, arithmetic and copies ran while one was open for 4% -> 5% of each run, Pallas kernels for 30% -> 19%
where the time goes in v3:
time: 182 us; the launch traced here: 180 us
  waiting for transfers between devices  66.5 us (37%)
  starting transfers between devices  56.1 us (31%)
  Pallas kernels  42.3 us (23%)
  local copies, waits for them, and re-layouts  9.81 us (5%)
  other arithmetic  4.29 us (2%)
    ppermute x4, waiting for transfers between devices, balanced_plan(): lax.ppermute(last_o, 'ctx', [(1, 3)])  42 us
    ppermute x4, starting transfers between devices, balanced_plan(): last_q = lax.ppermute(pieces[1], 'ctx', [(3, 1)])  31.8 us
    pallas_call x4, Pallas kernels, attend(): pl.pallas_call(partial(attend_kernel, genomes), out_shape=(jax.ShapeDtype...  19 us
    pallas_call x1, Pallas kernels, hyena(): pl.pallas_call(partial(hyena_kernel, genomes), out_shape=jax.ShapeDtypeSt...  15.9 us
    ppermute x4, waiting for transfers between devices, balanced_plan(): next_q = lax.ppermute(pieces[1], 'ctx', [(2, 1), (3, 2)])  14.2 us
    ppermute x4, waiting for transfers between devices, balanced_plan(): lax.ppermute(next_o, 'ctx', [(1, 2), (2, 3)])  9.25 us
    pallas_call x1, Pallas kernels, combine(): pl.pallas_call(partial(combine_kernel, genomes, heads), out_shape=jax.Sha...  7.33 us
    ppermute x4, starting transfers between devices, balanced_plan(): next_q = lax.ppermute(pieces[1], 'ctx', [(2, 1), (3, 2)])  6.16 us
  transfers between devices with their start and end apart: 25, of which 11 were waited for; matrix products, arithmetic and copies ran while one was open for 5% of the time, Pallas kernels for 19%

profile of v3, /device:TPU:30, one launch (start us, length us, event | category | flops | bytes accessed | tf_op | source)
XLA Modules:
  0.0 180.3 jit_solution(9896149271676764329)
XLA Ops:
  0.6 2.2 %multiply_convert_fusion = bf16[128,2048]{1,0:T(8,128)(2,1)} fusion(bf16[384,2048]{1,0:T(8,128)(2,1)} %value_ref.1, bf16[384,2048]{1,0:T(8,128)(2,1)} %key_ref.1), kind=kLoop, calls=%fused_computation | loop fusion | flops 1048576 | bytes 1572864 | tf_op jit(solution)/shard_map/convert_element_type | solution.py:449
  2.9 1.4 collective-permute-start
  4.3 1.2 fusion.2
  5.5 4.6 %collective-permute-start.8 = (bf16[384,512]{1,0:T(8,128)(2,1)}, bf16[384,512]{1,0:T(8,128)(2,1)S(1)}, u32[]{:S(2)}, u32[]{:S(2)}) collective-permute-start(bf16[384,512]{1,0:T(8,128)(2,1)} %get-tuple-element.70), channel_id=1, source_target_pairs={{12,4},{13,5},{14,6},{15,7},{28,20},{29,21},{30,22},{31,23}} | collective-permute-start | bytes 1179656 | tf_op jit(solution)/shard_map/ppermute | solution.py:465
  10.1 2.0 %collective-permute-start.7 = (bf16[384,512]{1,0:T(8,128)(2,1)}, bf16[384,512]{1,0:T(8,128)(2,1)}, u32[]{:S(2)}, u32[]{:S(2)}) collective-permute-start(bf16[384,512]{1,0:T(8,128)(2,1)} %get-tuple-element.70), channel_id=1, source_target_pairs={{8,4},{12,8},{9,5},{13,9},{10,6},{14,10},{11,7},{15,11},{24,20},{2... | collective-permute-start | bytes 1179656 | tf_op jit(solution)/shard_map/ppermute | solution.py:464
  12.1 1.2 fusion.1
  13.3 1.4 collective-permute-start.9
  14.7 1.5 slice.57
  16.2 1.4 slice.58
  18.2 1.5 maximum_convert_fusion.taps_ref
  19.7 15.9 %hyena.1.own_v = bf16[384,2048]{1,0:T(8,128)(2,1)} custom-call(s32[5]{0:T(128)} %pad_add_fusion.facts_ref, bf16[384,2048]{1,0:T(8,128)(2,1)} %query_ref.1, bf16[384,2048]{1,0:T(8,128)(2,1)} %key_ref.1, bf16[384,2048]{1,0:T(8,128)(2,1)} %value_ref.1, bf16[128,2048]{1,0:T(8,128)(2,1)} %collective-permute-done.halo_ref, ...), custom_call_target="tpu_custom_call" | custom-call | flops 3221225472 | bytes 6291456 | tf_op jit(solution)/shard_map/hyena/pallas_call | solution.py:206
  35.6 1.7 fusion
  37.3 0.7 collective-permute-start.10
  38.0 3.2 %collective-permute-start.2 = (bf16[384,512]{1,0:T(8,128)(2,1)S(1)}, bf16[384,512]{1,0:T(8,128)(2,1)S(1)}, u32[]{:S(2)}, u32[]{:S(2)}) collective-permute-start(bf16[384,512]{1,0:T(8,128)(2,1)S(1)} %copy-done.24), channel_id=1, source_target_pairs={{12,4},{13,5},{14,6},{15,7},{28,20},{29,21},{30,22},{31,23}} | collective-permute-start | bytes 1179656 | tf_op jit(solution)/shard_map/ppermute | solution.py:465
  41.2 1.3 collective-permute-start.1
  42.6 0.7 collective-permute-start.3
  43.3 0.8 collective-permute-start.4
  44.1 5.6 %attend.5 = (f32[384,512]{1,0:T(8,128)S(1)}, bf16[416,512]{1,0:T(8,128)(2,1)S(1)}, bf16[416,512]{1,0:T(8,128)(2,1)S(1)}, f32[8,384]{1,0:T(8,128)S(1)}) custom-call(s32[5]{0:T(128)S(1)} %copy-done.7, bf16[384,2048]{1,0:T(8,128)(2,1)S(1)} %copy-done, bf16[384,512]{1,0:T(8,128)(2,1)} %collective-permute-done.7.next_q, ...), custom_call_target="tpu_custom_call" | custom-call | flops 905969664 | bytes 4325376 | tf_op jit(solution)/shard_map/attend/pallas_call | solution.py:358
  49.8 0.8 collective-permute-start.21
  51.4 4.6 %collective-permute-done.1.next_q = bf16[384,512]{1,0:T(8,128)(2,1)S(1)} collective-permute-done((bf16[384,512]{1,0:T(8,128)(2,1)S(1)}, bf16[384,512]{1,0:T(8,128)(2,1)S(1)}, u32[]{:S(2)}, u32[]{:S(2)}) %collective-permute-start.1) | collective-permute-done | bytes 393248 | tf_op jit(solution)/shard_map/ppermute | solution.py:464
  56.0 4.5 %attend.4 = (f32[384,512]{1,0:T(8,128)S(1)}, bf16[416,512]{1,0:T(8,128)(2,1)S(1)}, bf16[416,512]{1,0:T(8,128)(2,1)S(1)}, f32[8,384]{1,0:T(8,128)S(1)}) custom-call(s32[5]{0:T(128)S(1)} %copy-done.7, bf16[384,2048]{1,0:T(8,128)(2,1)S(1)} %copy-done, bf16[384,512]{1,0:T(8,128)(2,1)S(1)} %collective-permute-done.1.next_q, ...), custom_call_target="tpu_custom_call" | custom-call | flops 905969664 | bytes 4325376 | tf_op jit(solution)/shard_map/attend/pallas_call | solution.py:358
  60.6 0.7 collective-permute-start.15
  61.9 19.5 %collective-permute-start.14 = (bf16[384,512]{1,0:T(8,128)(2,1)S(1)}, bf16[384,512]{1,0:T(8,128)(2,1)S(1)}, u32[]{:S(2)}, u32[]{:S(2)}) collective-permute-start(bf16[384,512]{1,0:T(8,128)(2,1)S(1)} %copy-done.21), channel_id=1, source_target_pairs={{12,4},{13,5},{14,6},{15,7},{28,20},{29,21},{30,22},{31,23}} | collective-permute-start | bytes 1179656 | tf_op jit(solution)/shard_map/ppermute | solution.py:465
  81.5 1.5 collective-permute-start.13
  83.0 4.5 %collective-permute-start.20 = (bf16[384,512]{1,0:T(8,128)(2,1)S(1)}, bf16[384,512]{1,0:T(8,128)(2,1)S(1)}, u32[]{:S(2)}, u32[]{:S(2)}) collective-permute-start(bf16[384,512]{1,0:T(8,128)(2,1)S(1)} %copy-done.20), channel_id=1, source_target_pairs={{12,4},{13,5},{14,6},{15,7},{28,20},{29,21},{30,22},{31,23}} | collective-permute-start | bytes 1179656 | tf_op jit(solution)/shard_map/ppermute | solution.py:465
  87.6 1.3 collective-permute-start.19
  88.9 1.3 collective-permute-start.5
  90.2 0.9 collective-permute-done.14.last_q
  91.0 1.3 collective-permute-start.6
  92.3 7.1 %collective-permute-done.13.next_q = bf16[384,512]{1,0:T(8,128)(2,1)S(1)} collective-permute-done((bf16[384,512]{1,0:T(8,128)(2,1)S(1)}, bf16[384,512]{1,0:T(8,128)(2,1)S(1)}, u32[]{:S(2)}, u32[]{:S(2)}) %collective-permute-start.13) | collective-permute-done | bytes 393248 | tf_op jit(solution)/shard_map/ppermute | solution.py:464
  99.5 1.3 collective-permute-start.11
  100.8 4.5 %attend.6 = (f32[384,512]{1,0:T(8,128)S(1)}, bf16[416,512]{1,0:T(8,128)(2,1)S(1)}, bf16[416,512]{1,0:T(8,128)(2,1)S(1)}, f32[8,384]{1,0:T(8,128)S(1)}) custom-call(s32[5]{0:T(128)S(1)} %copy-done.7, bf16[384,2048]{1,0:T(8,128)(2,1)S(1)} %copy-done, bf16[384,512]{1,0:T(8,128)(2,1)S(1)} %collective-permute-done.13.next_q, ...), custom_call_target="tpu_custom_call" | custom-call | flops 905969664 | bytes 4325376 | tf_op jit(solution)/shard_map/attend/pallas_call | solution.py:358
  105.9 1.3 collective-permute-start.12
  107.2 2.5 %collective-permute-done.19.next_q = bf16[384,512]{1,0:T(8,128)(2,1)S(1)} collective-permute-done((bf16[384,512]{1,0:T(8,128)(2,1)S(1)}, bf16[384,512]{1,0:T(8,128)(2,1)S(1)}, u32[]{:S(2)}, u32[]{:S(2)}) %collective-permute-start.19) | collective-permute-done | bytes 393248 | tf_op jit(solution)/shard_map/ppermute | solution.py:464
  109.7 1.3 collective-permute-start.17
  111.0 4.5 %attend.7 = (f32[384,512]{1,0:T(8,128)S(1)}, bf16[416,512]{1,0:T(8,128)(2,1)S(1)}, bf16[416,512]{1,0:T(8,128)(2,1)S(1)}, f32[8,384]{1,0:T(8,128)S(1)}) custom-call(s32[5]{0:T(128)S(1)} %copy-done.7, bf16[384,2048]{1,0:T(8,128)(2,1)S(1)} %copy-done, bf16[384,512]{1,0:T(8,128)(2,1)S(1)} %collective-permute-done.19.next_q, ...), custom_call_target="tpu_custom_call" | custom-call | flops 905969664 | bytes 4325376 | tf_op jit(solution)/shard_map/attend/pallas_call | solution.py:358
  115.5 0.9 copy-done.6
  117.0 1.3 collective-permute-start.18
  118.3 2.5 %collective-permute-done.6.refs_2_.refs_5_ = bf16[416,512]{1,0:T(8,128)(2,1)S(1)} collective-permute-done((bf16[416,512]{1,0:T(8,128)(2,1)S(1)}, bf16[416,512]{1,0:T(8,128)(2,1)S(1)}, u32[]{:S(2)}, u32[]{:S(2)}) %collective-permute-start.6) | collective-permute-done | bytes 426016 | tf_op jit(solution)/shard_map/ppermute | solution.py:476
  120.8 1.3 collective-permute-start.23
  122.0 4.0 %collective-permute-done.11.refs_7_.refs_10_ = bf16[416,512]{1,0:T(8,128)(2,1)S(1)} collective-permute-done((bf16[416,512]{1,0:T(8,128)(2,1)S(1)}, bf16[416,512]{1,0:T(8,128)(2,1)S(1)}, u32[]{:S(2)}, u32[]{:S(2)}) %collective-permute-start.11) | collective-permute-done | bytes 426016 | tf_op jit(solution)/shard_map/ppermute | solution.py:475
  126.1 1.3 collective-permute-start.24
  127.4 11.7 %collective-permute-done.12.refs_8_.refs_11_ = bf16[416,512]{1,0:T(8,128)(2,1)S(1)} collective-permute-done((bf16[416,512]{1,0:T(8,128)(2,1)S(1)}, bf16[416,512]{1,0:T(8,128)(2,1)S(1)}, u32[]{:S(2)}, u32[]{:S(2)}) %collective-permute-start.12) | collective-permute-done | bytes 426016 | tf_op jit(solution)/shard_map/ppermute | solution.py:476
  139.1 5.2 %collective-permute-done.17.refs_13_.refs_16_ = bf16[416,512]{1,0:T(8,128)(2,1)S(1)} collective-permute-done((bf16[416,512]{1,0:T(8,128)(2,1)S(1)}, bf16[416,512]{1,0:T(8,128)(2,1)S(1)}, u32[]{:S(2)}, u32[]{:S(2)}) %collective-permute-start.17) | collective-permute-done | bytes 426016 | tf_op jit(solution)/shard_map/ppermute | solution.py:475
  144.3 13.1 %collective-permute-done.18.refs_14_.refs_17_ = bf16[416,512]{1,0:T(8,128)(2,1)S(1)} collective-permute-done((bf16[416,512]{1,0:T(8,128)(2,1)S(1)}, bf16[416,512]{1,0:T(8,128)(2,1)S(1)}, u32[]{:S(2)}, u32[]{:S(2)}) %collective-permute-start.18) | collective-permute-done | bytes 426016 | tf_op jit(solution)/shard_map/ppermute | solution.py:476
  157.4 14.7 %collective-permute-done.24.refs_20_.refs_23_ = bf16[416,512]{1,0:T(8,128)(2,1)S(1)} collective-permute-done((bf16[416,512]{1,0:T(8,128)(2,1)S(1)}, bf16[416,512]{1,0:T(8,128)(2,1)S(1)}, u32[]{:S(2)}, u32[]{:S(2)}) %collective-permute-start.24) | collective-permute-done | bytes 426016 | tf_op jit(solution)/shard_map/ppermute | solution.py:476
  172.1 0.7 copy-done.19
  172.8 7.3 %combine.1 = bf16[384,2048]{1,0:T(8,128)(2,1)} custom-call(s32[5]{0:T(128)} %pad_add_fusion.facts_ref, f32[384,512]{1,0:T(8,128)} %copy-done.4, bf16[416,512]{1,0:T(8,128)(2,1)} %copy-done.12, bf16[416,512]{1,0:T(8,128)(2,1)} %copy-done.13, f32[8,384]{1,0:T(8,128)} %copy-done.9, bf16[416,512]{1,0:T(8,128)(2,1)} %copy-done.12, bf16[416,512]{1,0:T(8,128)(2,1)} %copy-done.13, ...), custom_call_target="tpu_custom_call" | custom-call | flops 12582912 | bytes 7864320 | tf_op jit(solution)/shard_map/combine/pallas_call | solution.py:423
  (70 shorter events, 3.4 us)
Async XLA Ops:
  0.6 3.7 %copy-start = (bf16[384,2048]{1,0:T(8,128)(2,1)S(1)}, bf16[384,2048]{1,0:T(8,128)(2,1)}, u32[]{:S(2)}) copy-start(bf16[384,2048]{1,0:T(8,128)(2,1)} %own_q.7) | copy-start | bytes 4718596
  2.9 9.3 %copy-start.1 = (bf16[384,2048]{1,0:T(8,128)(2,1)S(1)}, bf16[384,2048]{1,0:T(8,128)(2,1)}, u32[]{:S(2)}) copy-start(bf16[384,2048]{1,0:T(8,128)(2,1)} %own_k.7) | copy-start | bytes 4718596
  2.9 16.8 %collective-permute-start = (bf16[128,2048]{1,0:T(8,128)(2,1)}, bf16[128,2048]{1,0:T(8,128)(2,1)}, u32[]{:S(2)}, u32[]{:S(2)}) collective-permute-start(bf16[128,2048]{1,0:T(8,128)(2,1)} %multiply_convert_fusion), channel_id=1, source_target_pairs={{0,4},{4,8},{8,12},{1,5},{5,9},{9,13},{2,6},{6,10},{10,14},{3,7},{... | collective-permute-start | bytes 1572872 | tf_op jit(solution)/shard_map/ppermute | solution.py:17
  5.5 12.1 %copy-start.26 = (s32[4]{0:T(128)S(1)}, s32[4]{0:T(128)}, u32[]{:S(2)}) copy-start(s32[4]{0:T(128)} %param.15) | copy-start | bytes 52
  5.5 35.7 %collective-permute-start.8 = (bf16[384,512]{1,0:T(8,128)(2,1)}, bf16[384,512]{1,0:T(8,128)(2,1)S(1)}, u32[]{:S(2)}, u32[]{:S(2)}) collective-permute-start(bf16[384,512]{1,0:T(8,128)(2,1)} %get-tuple-element.70), channel_id=1, source_target_pairs={{12,4},{13,5},{14,6},{15,7},{28,20},{29,21},{30,22},{31,23}} | collective-permute-start | bytes 1179656 | tf_op jit(solution)/shard_map/ppermute | solution.py:465
  10.1 32.5 %collective-permute-start.7 = (bf16[384,512]{1,0:T(8,128)(2,1)}, bf16[384,512]{1,0:T(8,128)(2,1)}, u32[]{:S(2)}, u32[]{:S(2)}) collective-permute-start(bf16[384,512]{1,0:T(8,128)(2,1)} %get-tuple-element.70), channel_id=1, source_target_pairs={{8,4},{12,8},{9,5},{13,9},{10,6},{14,10},{11,7},{15,11},{24,20},{2... | collective-permute-start | bytes 1179656 | tf_op jit(solution)/shard_map/ppermute | solution.py:464
  13.3 29.9 %collective-permute-start.9 = (bf16[384,512]{1,0:T(8,128)(2,1)}, bf16[384,512]{1,0:T(8,128)(2,1)}, u32[]{:S(2)}, u32[]{:S(2)}) collective-permute-start(bf16[384,512]{1,0:T(8,128)(2,1)} %get-tuple-element.66), channel_id=1, source_target_pairs={{0,4},{1,5},{2,6},{3,7},{16,20},{17,21},{18,22},{19,23}} | collective-permute-start | bytes 1179656 | tf_op jit(solution)/shard_map/ppermute | solution.py:463
  35.6 2.4 %copy-start.24 = (bf16[384,512]{1,0:T(8,128)(2,1)S(1)}, bf16[384,512]{1,0:T(8,128)(2,1)}, u32[]{:S(2)}) copy-start(bf16[384,512]{1,0:T(8,128)(2,1)} %get-tuple-element.72) | copy-start | bytes 1179652
  35.6 7.0 %copy-start.25 = (bf16[384,512]{1,0:T(8,128)(2,1)S(1)}, bf16[384,512]{1,0:T(8,128)(2,1)}, u32[]{:S(2)}) copy-start(bf16[384,512]{1,0:T(8,128)(2,1)} %get-tuple-element.68) | copy-start | bytes 1179652
  35.6 8.5 %copy-start.2 = (bf16[384,2048]{1,0:T(8,128)(2,1)S(1)}, bf16[384,2048]{1,0:T(8,128)(2,1)}, u32[]{:S(2)}) copy-start(bf16[384,2048]{1,0:T(8,128)(2,1)} %hyena.1.own_v) | copy-start | bytes 4718596
  35.6 8.5 %copy-start.7 = (s32[5]{0:T(128)S(1)}, s32[5]{0:T(128)}, u32[]{:S(2)}) copy-start(s32[5]{0:T(128)} %pad_add_fusion.facts_ref) | copy-start | bytes 64
  37.3 6.8 %collective-permute-start.10 = (bf16[384,512]{1,0:T(8,128)(2,1)S(1)}, bf16[384,512]{1,0:T(8,128)(2,1)S(1)}, u32[]{:S(2)}, u32[]{:S(2)}) collective-permute-start(bf16[384,512]{1,0:T(8,128)(2,1)S(1)} %get-tuple-element.62), channel_id=1, source_target_pairs={{0,4},{1,5},{2,6},{3,7},{16,20},{17,21},{18,22},{19,23}} | collective-permute-start | bytes 1179656 | tf_op jit(solution)/shard_map/ppermute | solution.py:466
  38.0 12.7 %collective-permute-start.2 = (bf16[384,512]{1,0:T(8,128)(2,1)S(1)}, bf16[384,512]{1,0:T(8,128)(2,1)S(1)}, u32[]{:S(2)}, u32[]{:S(2)}) collective-permute-start(bf16[384,512]{1,0:T(8,128)(2,1)S(1)} %copy-done.24), channel_id=1, source_target_pairs={{12,4},{13,5},{14,6},{15,7},{28,20},{29,21},{30,22},{31,23}} | collective-permute-start | bytes 1179656 | tf_op jit(solution)/shard_map/ppermute | solution.py:465
  41.2 14.8 %collective-permute-start.1 = (bf16[384,512]{1,0:T(8,128)(2,1)S(1)}, bf16[384,512]{1,0:T(8,128)(2,1)S(1)}, u32[]{:S(2)}, u32[]{:S(2)}) collective-permute-start(bf16[384,512]{1,0:T(8,128)(2,1)S(1)} %copy-done.24), channel_id=1, source_target_pairs={{8,4},{12,8},{9,5},{13,9},{10,6},{14,10},{11,7},{15,11},{24,20},{2... | collective-permute-start | bytes 1179656 | tf_op jit(solution)/shard_map/ppermute | solution.py:464
  42.6 13.4 %collective-permute-start.3 = (bf16[384,512]{1,0:T(8,128)(2,1)S(1)}, bf16[384,512]{1,0:T(8,128)(2,1)S(1)}, u32[]{:S(2)}, u32[]{:S(2)}) collective-permute-start(bf16[384,512]{1,0:T(8,128)(2,1)S(1)} %copy-done.25), channel_id=1, source_target_pairs={{0,4},{1,5},{2,6},{3,7},{16,20},{17,21},{18,22},{19,23}} | collective-permute-start | bytes 1179656 | tf_op jit(solution)/shard_map/ppermute | solution.py:463
  43.3 6.5 %copy-start.23 = (bf16[384,512]{1,0:T(8,128)(2,1)S(1)}, bf16[384,512]{1,0:T(8,128)(2,1)}, u32[]{:S(2)}) copy-start(bf16[384,512]{1,0:T(8,128)(2,1)} %get-tuple-element.56) | copy-start | bytes 1179652
  43.3 12.7 %collective-permute-start.4 = (bf16[384,512]{1,0:T(8,128)(2,1)S(1)}, bf16[384,512]{1,0:T(8,128)(2,1)S(1)}, u32[]{:S(2)}, u32[]{:S(2)}) collective-permute-start(bf16[384,512]{1,0:T(8,128)(2,1)S(1)} %get-tuple-element.64), channel_id=1, source_target_pairs={{0,4},{1,5},{2,6},{3,7},{16,20},{17,21},{18,22},{19,23}} | collective-permute-start | bytes 1179656 | tf_op jit(solution)/shard_map/ppermute | solution.py:466
  49.7 10.8 %copy-start.3 = (f32[384,512]{1,0:T(8,128)}, f32[384,512]{1,0:T(8,128)S(1)}, u32[]{:S(2)}) copy-start(f32[384,512]{1,0:T(8,128)S(1)} %get-tuple-element.44.refs_6_) | copy-start | bytes 2359300
  49.7 10.8 %copy-start.8 = (f32[8,384]{1,0:T(8,128)}, f32[8,384]{1,0:T(8,128)S(1)}, u32[]{:S(2)}) copy-start(f32[8,384]{1,0:T(8,128)S(1)} %get-tuple-element.47.refs_9_) | copy-start | bytes 36868
  49.7 10.8 %copy-start.22 = (bf16[384,512]{1,0:T(8,128)(2,1)S(1)}, bf16[384,512]{1,0:T(8,128)(2,1)}, u32[]{:S(2)}) copy-start(bf16[384,512]{1,0:T(8,128)(2,1)} %get-tuple-element.49) | copy-start | bytes 1179652
  49.7 12.2 %copy-start.21 = (bf16[384,512]{1,0:T(8,128)(2,1)S(1)}, bf16[384,512]{1,0:T(8,128)(2,1)}, u32[]{:S(2)}) copy-start(bf16[384,512]{1,0:T(8,128)(2,1)} %get-tuple-element.48) | copy-start | bytes 1179652
  49.7 33.2 %copy-start.20 = (bf16[384,512]{1,0:T(8,128)(2,1)S(1)}, bf16[384,512]{1,0:T(8,128)(2,1)}, u32[]{:S(2)}) copy-start(bf16[384,512]{1,0:T(8,128)(2,1)} %get-tuple-element.55) | copy-start | bytes 1179652
  49.8 31.7 %collective-permute-start.21 = (bf16[384,512]{1,0:T(8,128)(2,1)S(1)}, bf16[384,512]{1,0:T(8,128)(2,1)S(1)}, u32[]{:S(2)}, u32[]{:S(2)}) collective-permute-start(bf16[384,512]{1,0:T(8,128)(2,1)S(1)} %copy-done.23), channel_id=1, source_target_pairs={{0,4},{1,5},{2,6},{3,7},{16,20},{17,21},{18,22},{19,23}} | collective-permute-start | bytes 1179656 | tf_op jit(solution)/shard_map/ppermute | solution.py:463
  50.7 32.2 %collective-permute-start.22 = (bf16[384,512]{1,0:T(8,128)(2,1)S(1)}, bf16[384,512]{1,0:T(8,128)(2,1)S(1)}, u32[]{:S(2)}, u32[]{:S(2)}) collective-permute-start(bf16[384,512]{1,0:T(8,128)(2,1)S(1)} %get-tuple-element.57), channel_id=1, source_target_pairs={{0,4},{1,5},{2,6},{3,7},{16,20},{17,21},{18,22},{19,23}} | collective-permute-start | bytes 1179656 | tf_op jit(solution)/shard_map/ppermute | solution.py:466
  60.5 44.7 %copy-start.4 = (f32[384,512]{1,0:T(8,128)}, f32[384,512]{1,0:T(8,128)S(1)}, u32[]{:S(2)}) copy-start(f32[384,512]{1,0:T(8,128)S(1)} %get-tuple-element.36.refs_0_) | copy-start | bytes 2359300
  60.5 44.7 %copy-start.9 = (f32[8,384]{1,0:T(8,128)}, f32[8,384]{1,0:T(8,128)S(1)}, u32[]{:S(2)}) copy-start(f32[8,384]{1,0:T(8,128)S(1)} %get-tuple-element.39.refs_3_) | copy-start | bytes 36868
  60.6 27.0 %collective-permute-start.15 = (bf16[384,512]{1,0:T(8,128)(2,1)S(1)}, bf16[384,512]{1,0:T(8,128)(2,1)S(1)}, u32[]{:S(2)}, u32[]{:S(2)}) collective-permute-start(bf16[384,512]{1,0:T(8,128)(2,1)S(1)} %copy-done.22), channel_id=1, source_target_pairs={{0,4},{1,5},{2,6},{3,7},{16,20},{17,21},{18,22},{19,23}} | collective-permute-start | bytes 1179656 | tf_op jit(solution)/shard_map/ppermute | solution.py:463
  61.2 27.6 %collective-permute-start.16 = (bf16[384,512]{1,0:T(8,128)(2,1)S(1)}, bf16[384,512]{1,0:T(8,128)(2,1)S(1)}, u32[]{:S(2)}, u32[]{:S(2)}) collective-permute-start(bf16[384,512]{1,0:T(8,128)(2,1)S(1)} %get-tuple-element.50), channel_id=1, source_target_pairs={{0,4},{1,5},{2,6},{3,7},{16,20},{17,21},{18,22},{19,23}} | collective-permute-start | bytes 1179656 | tf_op jit(solution)/shard_map/ppermute | solution.py:466
  61.9 29.1 %collective-permute-start.14 = (bf16[384,512]{1,0:T(8,128)(2,1)S(1)}, bf16[384,512]{1,0:T(8,128)(2,1)S(1)}, u32[]{:S(2)}, u32[]{:S(2)}) collective-permute-start(bf16[384,512]{1,0:T(8,128)(2,1)S(1)} %copy-done.21), channel_id=1, source_target_pairs={{12,4},{13,5},{14,6},{15,7},{28,20},{29,21},{30,22},{31,23}} | collective-permute-start | bytes 1179656 | tf_op jit(solution)/shard_map/ppermute | solution.py:465
  81.5 18.0 %collective-permute-start.13 = (bf16[384,512]{1,0:T(8,128)(2,1)S(1)}, bf16[384,512]{1,0:T(8,128)(2,1)S(1)}, u32[]{:S(2)}, u32[]{:S(2)}) collective-permute-start(bf16[384,512]{1,0:T(8,128)(2,1)S(1)} %copy-done.21), channel_id=1, source_target_pairs={{8,4},{12,8},{9,5},{13,9},{10,6},{14,10},{11,7},{15,11},{24,20},{2... | collective-permute-start | bytes 1179656 | tf_op jit(solution)/shard_map/ppermute | solution.py:464
  83.0 22.9 %collective-permute-start.20 = (bf16[384,512]{1,0:T(8,128)(2,1)S(1)}, bf16[384,512]{1,0:T(8,128)(2,1)S(1)}, u32[]{:S(2)}, u32[]{:S(2)}) collective-permute-start(bf16[384,512]{1,0:T(8,128)(2,1)S(1)} %copy-done.20), channel_id=1, source_target_pairs={{12,4},{13,5},{14,6},{15,7},{28,20},{29,21},{30,22},{31,23}} | collective-permute-start | bytes 1179656 | tf_op jit(solution)/shard_map/ppermute | solution.py:465
  87.6 22.1 %collective-permute-start.19 = (bf16[384,512]{1,0:T(8,128)(2,1)S(1)}, bf16[384,512]{1,0:T(8,128)(2,1)S(1)}, u32[]{:S(2)}, u32[]{:S(2)}) collective-permute-start(bf16[384,512]{1,0:T(8,128)(2,1)S(1)} %copy-done.20), channel_id=1, source_target_pairs={{8,4},{12,8},{9,5},{13,9},{10,6},{14,10},{11,7},{15,11},{24,20},{2... | collective-permute-start | bytes 1179656 | tf_op jit(solution)/shard_map/ppermute | solution.py:464
  88.9 28.1 %collective-permute-start.5 = (bf16[416,512]{1,0:T(8,128)(2,1)S(1)}, bf16[416,512]{1,0:T(8,128)(2,1)S(1)}, u32[]{:S(2)}, u32[]{:S(2)}) collective-permute-start(bf16[416,512]{1,0:T(8,128)(2,1)S(1)} %get-tuple-element.37), channel_id=1, source_target_pairs={{4,8},{8,12},{5,9},{9,13},{6,10},{10,14},{7,11},{11,15},{20,24},{2... | collective-permute-start | bytes 1277960 | tf_op jit(solution)/shard_map/ppermute | solution.py:475
  91.0 29.7 %collective-permute-start.6 = (bf16[416,512]{1,0:T(8,128)(2,1)S(1)}, bf16[416,512]{1,0:T(8,128)(2,1)S(1)}, u32[]{:S(2)}, u32[]{:S(2)}) collective-permute-start(bf16[416,512]{1,0:T(8,128)(2,1)S(1)} %get-tuple-element.38), channel_id=1, source_target_pairs={{4,12},{5,13},{6,14},{7,15},{20,28},{21,29},{22,30},{23,31}} | collective-permute-start | bytes 1277960 | tf_op jit(solution)/shard_map/ppermute | solution.py:476
  99.5 26.6 %collective-permute-start.11 = (bf16[416,512]{1,0:T(8,128)(2,1)S(1)}, bf16[416,512]{1,0:T(8,128)(2,1)S(1)}, u32[]{:S(2)}, u32[]{:S(2)}) collective-permute-start(bf16[416,512]{1,0:T(8,128)(2,1)S(1)} %get-tuple-element.45), channel_id=1, source_target_pairs={{4,8},{8,12},{5,9},{9,13},{6,10},{10,14},{7,11},{11,15},{20,24},{2... | collective-permute-start | bytes 1277960 | tf_op jit(solution)/shard_map/ppermute | solution.py:475
  105.9 9.6 %copy-start.5 = (f32[384,512]{1,0:T(8,128)}, f32[384,512]{1,0:T(8,128)S(1)}, u32[]{:S(2)}) copy-start(f32[384,512]{1,0:T(8,128)S(1)} %get-tuple-element.51.refs_12_) | copy-start | bytes 2359300
  105.9 33.2 %collective-permute-start.12 = (bf16[416,512]{1,0:T(8,128)(2,1)S(1)}, bf16[416,512]{1,0:T(8,128)(2,1)S(1)}, u32[]{:S(2)}, u32[]{:S(2)}) collective-permute-start(bf16[416,512]{1,0:T(8,128)(2,1)S(1)} %get-tuple-element.46), channel_id=1, source_target_pairs={{4,12},{5,13},{6,14},{7,15},{20,28},{21,29},{22,30},{23,31}} | collective-permute-start | bytes 1277960 | tf_op jit(solution)/shard_map/ppermute | solution.py:476
  109.7 34.6 %collective-permute-start.17 = (bf16[416,512]{1,0:T(8,128)(2,1)S(1)}, bf16[416,512]{1,0:T(8,128)(2,1)S(1)}, u32[]{:S(2)}, u32[]{:S(2)}) collective-permute-start(bf16[416,512]{1,0:T(8,128)(2,1)S(1)} %get-tuple-element.52), channel_id=1, source_target_pairs={{4,8},{8,12},{5,9},{9,13},{6,10},{10,14},{7,11},{11,15},{20,24},{2... | collective-permute-start | bytes 1277960 | tf_op jit(solution)/shard_map/ppermute | solution.py:475
  117.0 55.1 %copy-start.12 = (bf16[416,512]{1,0:T(8,128)(2,1)}, bf16[416,512]{1,0:T(8,128)(2,1)S(1)}, u32[]{:S(2)}) copy-start(bf16[416,512]{1,0:T(8,128)(2,1)S(1)} %collective-permute-done.5.refs_1_.refs_4_) | copy-start | bytes 1277956
  117.0 40.4 %collective-permute-start.18 = (bf16[416,512]{1,0:T(8,128)(2,1)S(1)}, bf16[416,512]{1,0:T(8,128)(2,1)S(1)}, u32[]{:S(2)}, u32[]{:S(2)}) collective-permute-start(bf16[416,512]{1,0:T(8,128)(2,1)S(1)} %get-tuple-element.53), channel_id=1, source_target_pairs={{4,12},{5,13},{6,14},{7,15},{20,28},{21,29},{22,30},{23,31}} | collective-permute-start | bytes 1277960 | tf_op jit(solution)/shard_map/ppermute | solution.py:476
  120.8 51.3 %copy-start.13 = (bf16[416,512]{1,0:T(8,128)(2,1)}, bf16[416,512]{1,0:T(8,128)(2,1)S(1)}, u32[]{:S(2)}) copy-start(bf16[416,512]{1,0:T(8,128)(2,1)S(1)} %collective-permute-done.6.refs_2_.refs_5_) | copy-start | bytes 1277956
  120.8 36.6 %collective-permute-start.23 = (bf16[416,512]{1,0:T(8,128)(2,1)S(1)}, bf16[416,512]{1,0:T(8,128)(2,1)S(1)}, u32[]{:S(2)}, u32[]{:S(2)}) collective-permute-start(bf16[416,512]{1,0:T(8,128)(2,1)S(1)} %get-tuple-element.59), channel_id=1, source_target_pairs={{4,8},{8,12},{5,9},{9,13},{6,10},{10,14},{7,11},{11,15},{20,24},{2... | collective-permute-start | bytes 1277960 | tf_op jit(solution)/shard_map/ppermute | solution.py:475
  126.1 46.0 %copy-start.14 = (bf16[416,512]{1,0:T(8,128)(2,1)}, bf16[416,512]{1,0:T(8,128)(2,1)S(1)}, u32[]{:S(2)}) copy-start(bf16[416,512]{1,0:T(8,128)(2,1)S(1)} %collective-permute-done.11.refs_7_.refs_10_) | copy-start | bytes 1277956
  126.1 46.0 %collective-permute-start.24 = (bf16[416,512]{1,0:T(8,128)(2,1)S(1)}, bf16[416,512]{1,0:T(8,128)(2,1)S(1)}, u32[]{:S(2)}, u32[]{:S(2)}) collective-permute-start(bf16[416,512]{1,0:T(8,128)(2,1)S(1)} %get-tuple-element.60), channel_id=1, source_target_pairs={{4,12},{5,13},{6,14},{7,15},{20,28},{21,29},{22,30},{23,31}} | collective-permute-start | bytes 1277960 | tf_op jit(solution)/shard_map/ppermute | solution.py:476
  139.1 33.0 %copy-start.15 = (bf16[416,512]{1,0:T(8,128)(2,1)}, bf16[416,512]{1,0:T(8,128)(2,1)S(1)}, u32[]{:S(2)}) copy-start(bf16[416,512]{1,0:T(8,128)(2,1)S(1)} %collective-permute-done.12.refs_8_.refs_11_) | copy-start | bytes 1277956
  144.3 27.8 %copy-start.16 = (bf16[416,512]{1,0:T(8,128)(2,1)}, bf16[416,512]{1,0:T(8,128)(2,1)S(1)}, u32[]{:S(2)}) copy-start(bf16[416,512]{1,0:T(8,128)(2,1)S(1)} %collective-permute-done.17.refs_13_.refs_16_) | copy-start | bytes 1277956
  157.4 14.8 %copy-start.17 = (bf16[416,512]{1,0:T(8,128)(2,1)}, bf16[416,512]{1,0:T(8,128)(2,1)S(1)}, u32[]{:S(2)}) copy-start(bf16[416,512]{1,0:T(8,128)(2,1)S(1)} %collective-permute-done.18.refs_14_.refs_17_) | copy-start | bytes 1277956
  157.4 14.8 %copy-start.18 = (bf16[416,512]{1,0:T(8,128)(2,1)}, bf16[416,512]{1,0:T(8,128)(2,1)S(1)}, u32[]{:S(2)}) copy-start(bf16[416,512]{1,0:T(8,128)(2,1)S(1)} %collective-permute-done.23.refs_19_.refs_22_) | copy-start | bytes 1277956
  (4 other events, 2.9 us)
